TPU v7x, 32 devices: a whole 2x2x4 slice. The times are simulated.
32 devices in a mesh: round: 4 (over z), stab: 8 (over y, x, core).
Axes of the slice: x: 2, y: 2, z: 4, core: 2. Of those that a mesh axis runs over, the one named last changes fastest.
Arguments:
- inputs: bfloat16 [32, 896, 512], P('round', 'stab'), may hold values from -6 to 6
- labels: int32 [32, 896], P('round', 'stab'), may hold values 0 or 1
- neighbours: int32 [224, 16], replicated, may hold values from 0 to 209, as said below
- space_in_weights: bfloat16 [512, 1536], replicated
- space_out_weights: bfloat16 [512, 512], replicated, may hold values from -0.25 to 0.25
- space_gain: float32 [512], replicated, may hold values from 0.5 to 1.5
- time_in_weights: bfloat16 [512, 1536], replicated
- time_out_weights: bfloat16 [512, 512], replicated, may hold values from -0.25 to 0.25
- time_gain: float32 [512], replicated, may hold values from 0.5 to 1.5
- readout: float32 [512], replicated, may hold values from -1 to 1
Outputs:
- grad_inputs: float32 [32, 896, 512], P('round', 'stab')
Inputs may be any that keep to these rules, and one draw needn't show every extreme that they name: `neighbours`: row b lists 16 distinct blocks below 210; each such block b lists itself.
All inputs are finite; a program needn't handle non-finite values. No bound on the sum of `labels` on one device may be relied on, other than what follows from the above.
Results may differ from a plain program's by a relative error of at most 0.0085.
Values may be sent and summed in bfloat16 or wider, within the bound.
A program may use at most 320 MiB of HBM per device.

v0:
```python
import jax
import jax.numpy as jnp
from jax import lax
from jax.sharding import PartitionSpec as P

HEADS = 8
HEAD_DIM = 64
STABS_REAL = 840
BLOCK = 4


EPSILON = 1e-06
MASKED_SCORE = -1e30


def contract(form, first_operand, second_operand):
    return jnp.einsum(form, first_operand, second_operand, preferred_element_type=jnp.float32)


def norm_rows(hidden, gain):
    inverse = lax.rsqrt(jnp.mean(hidden * hidden, axis=-1, keepdims=True) + EPSILON)
    return ((hidden * inverse * gain).astype(jnp.bfloat16), inverse)


def norm_back(hidden, inverse, gain, upstream):
    scaled = upstream * gain
    inner = jnp.mean(hidden * scaled, axis=-1, keepdims=True)
    return inverse * scaled - hidden * inverse * inverse * inverse * inner


def block_rows_of(field, neighbours):
    depth = field.shape[-1]
    blocked = field.reshape(-1, BLOCK, depth)
    return blocked[neighbours].reshape(neighbours.shape[0], -1, depth)


def spread_rows(near_grad, neighbours):
    depth = near_grad.shape[-1]
    block_count = neighbours.shape[0]
    pieces = near_grad.reshape(block_count, neighbours.shape[1], BLOCK, depth)
    summed = jnp.zeros((block_count, BLOCK, depth), near_grad.dtype).at[neighbours].add(pieces)
    return summed.reshape(-1, depth)


def space_scores(queries, key_rows, neighbours):
    depth = queries.shape[-1]
    factor = depth ** (-0.5)
    query_blocks = queries.reshape(-1, BLOCK, depth)
    near_keys = block_rows_of(key_rows, neighbours)
    return (
        contract("nid,njd->nij", query_blocks, near_keys) * factor,
        query_blocks,
        near_keys,
        factor,
    )


def space_forward(queries, key_rows, values, neighbours):
    scores, query_blocks, near_keys, factor = space_scores(queries, key_rows, neighbours)
    highest = jnp.max(scores, axis=-1, keepdims=True)
    logsum = highest + jnp.log(jnp.sum(jnp.exp(scores - highest), axis=-1, keepdims=True))
    weights = jnp.exp(scores - logsum).astype(jnp.bfloat16)
    attended = contract("nij,njd->nid", weights, block_rows_of(values, neighbours)).astype(
        jnp.bfloat16
    )
    return (attended.reshape(queries.shape), logsum)


def space_backward(queries, key_rows, values, neighbours, attended, grad_rows, logsum):
    scores, query_blocks, near_keys, factor = space_scores(queries, key_rows, neighbours)
    near_values = block_rows_of(values, neighbours)
    probability = jnp.exp(scores - logsum)
    weights = probability.astype(jnp.bfloat16)
    grad_blocks = grad_rows.reshape(query_blocks.shape)
    spread = jnp.sum(grad_rows.astype(jnp.float32) * attended.astype(jnp.float32), axis=-1).reshape(
        -1, BLOCK
    )[:, :, None]
    grad_near_values = contract("nij,nid->njd", weights, grad_blocks)
    grad_weights = contract("nid,njd->nij", grad_blocks, near_values)
    grad_scores = (probability * (grad_weights - spread) * factor).astype(jnp.bfloat16)
    grad_queries = contract("nij,njd->nid", grad_scores, near_keys).reshape(queries.shape)
    grad_near_keys = contract("nij,nid->njd", grad_scores, query_blocks)
    return (
        grad_queries,
        spread_rows(grad_near_keys, neighbours),
        spread_rows(grad_near_values, neighbours),
    )


def causal_scores(queries, key_rows, query_offset, key_offset):
    query_len, pair_count, span = queries.shape
    key_len = key_rows.shape[0]
    query_heads = queries.reshape(query_len, pair_count, 2, span // 2)
    key_heads = key_rows.reshape(key_len, pair_count, 2, span // 2)
    factor = (span // 2) ** (-0.5)
    scores = contract("qphd,kphd->phqk", query_heads, key_heads) * factor
    allowed = (query_offset + jnp.arange(query_len))[:, None] >= (key_offset + jnp.arange(key_len))[
        None, :
    ]
    return (jnp.where(allowed, scores, MASKED_SCORE), query_heads, key_heads, factor)


def time_forward(queries, key_rows, values, query_offset, key_offset):
    scores, query_heads, key_heads, factor = causal_scores(
        queries, key_rows, query_offset, key_offset
    )
    value_heads = values.reshape(key_heads.shape)
    highest = jnp.max(scores, axis=-1, keepdims=True)
    logsum = highest + jnp.log(jnp.sum(jnp.exp(scores - highest), axis=-1, keepdims=True))
    weights = jnp.exp(scores - logsum).astype(jnp.bfloat16)
    attended = contract("phqk,kphd->qphd", weights, value_heads).astype(jnp.bfloat16)
    return (attended.reshape(queries.shape), jnp.transpose(logsum[..., 0], (2, 0, 1)))


def delta_rows(attended, grad_rows):
    product = attended.astype(jnp.float32) * grad_rows.astype(jnp.float32)
    return jnp.sum(product.reshape(attended.shape[0], attended.shape[1], 2, -1), axis=-1)


def time_backward(queries, key_rows, values, grad_rows, logsum, spread, query_offset, key_offset):
    scores, query_heads, key_heads, factor = causal_scores(
        queries, key_rows, query_offset, key_offset
    )
    value_heads = values.reshape(key_heads.shape)
    grad_heads = grad_rows.reshape(query_heads.shape)
    probability = jnp.exp(scores - jnp.transpose(logsum, (1, 2, 0))[..., None])
    weights = probability.astype(jnp.bfloat16)
    grad_values = contract("phqk,qphd->kphd", weights, grad_heads)
    grad_weights = contract("qphd,kphd->phqk", grad_heads, value_heads)
    grad_scores = (
        probability * (grad_weights - jnp.transpose(spread, (1, 2, 0))[..., None]) * factor
    ).astype(jnp.bfloat16)
    grad_queries = contract("phqk,kphd->qphd", grad_scores, key_heads)
    grad_keys = contract("phqk,qphd->kphd", grad_scores, query_heads)
    return (
        grad_queries.reshape(queries.shape),
        grad_keys.reshape(key_rows.shape),
        grad_values.reshape(key_rows.shape),
    )


def time_key_side(queries_all, key_rows, values, grad_all, logsum_all, spread_all, key_offset):
    query_len, pair_count, span = queries_all.shape
    key_len = key_rows.shape[0]
    query_heads = queries_all.reshape(query_len, pair_count, 2, span // 2)
    key_heads = key_rows.reshape(key_len, pair_count, 2, span // 2)
    value_heads = values.reshape(key_heads.shape)
    grad_heads = grad_all.reshape(query_heads.shape)
    factor = (span // 2) ** (-0.5)
    scores = contract("qphd,kphd->phkq", query_heads, key_heads) * factor
    allowed = jnp.arange(query_len)[None, :] >= (key_offset + jnp.arange(key_len))[:, None]
    scores = jnp.where(allowed, scores, MASKED_SCORE)
    probability = jnp.exp(scores - jnp.transpose(logsum_all, (1, 2, 0))[:, :, None, :])
    weights = probability.astype(jnp.bfloat16)
    grad_values = contract("phkq,qphd->kphd", weights, grad_heads)
    grad_weights = contract("qphd,kphd->phkq", grad_heads, value_heads)
    grad_scores = (
        probability * (grad_weights - jnp.transpose(spread_all, (1, 2, 0))[:, :, None, :]) * factor
    ).astype(jnp.bfloat16)
    grad_keys = contract("phkq,qphd->kphd", grad_scores, query_heads)
    return (grad_keys.reshape(key_rows.shape), grad_values.reshape(key_rows.shape))


def readout_grad(after_time, readout, targets, real_mask):
    logits = jnp.sum(after_time * readout, axis=-1)
    grad_logits = (jax.nn.sigmoid(logits) - targets.astype(jnp.float32)) * real_mask
    return grad_logits[..., None] * readout


def body(
    inputs,
    labels,
    neighbours,
    space_in_weights,
    space_out_weights,
    space_gain,
    time_in_weights,
    time_out_weights,
    time_gain,
    readout,
):
    rounds_here, stabs_here, features = inputs.shape
    space_four = space_in_weights.reshape(features, 3, HEADS, HEAD_DIM)
    space_three = space_out_weights.reshape(HEADS, HEAD_DIM, features)
    time_three = time_in_weights.reshape(features, 3, features)
    widened = inputs.astype(jnp.float32)
    normed, inverse = norm_rows(widened, space_gain)
    triple = contract("rsd,dchk->crhsk", normed, space_four).astype(jnp.bfloat16)
    triple = triple.reshape(3, rounds_here * HEADS, stabs_here, HEAD_DIM)
    query_space, key_space, value_space = (
        lax.all_to_all(triple[0], "stab", split_axis=0, concat_axis=1, tiled=True),
        lax.all_to_all(triple[1], "stab", split_axis=0, concat_axis=1, tiled=True),
        lax.all_to_all(triple[2], "stab", split_axis=0, concat_axis=1, tiled=True),
    )
    attend = jax.vmap(space_forward, in_axes=(0, 0, 0, None))
    attended_space, logsum_space = attend(query_space, key_space, value_space, neighbours)
    mixed_space = lax.all_to_all(attended_space, "stab", split_axis=1, concat_axis=0, tiled=True)
    mixed_space = mixed_space.reshape(rounds_here, HEADS, stabs_here, HEAD_DIM)
    after_space = widened + contract("rhsk,hkd->rsd", mixed_space, space_three)
    normed_time, inverse_time = norm_rows(after_space, time_gain)
    pair_count = stabs_here * HEADS // 2
    trio = contract("rsd,dce->crse", normed_time, time_three).astype(jnp.bfloat16)
    trio = trio.reshape(3, rounds_here, pair_count, 2 * HEAD_DIM)
    queries, key_rows, values = (trio[0], trio[1], trio[2])
    offset = lax.axis_index("round") * rounds_here
    keys_all, values_all = (
        lax.all_gather(key_rows, "round", axis=0, tiled=True),
        lax.all_gather(values, "round", axis=0, tiled=True),
    )
    attended_time, logsum_time = time_forward(queries, keys_all, values_all, offset, 0)
    after_time = after_space + jnp.dot(
        attended_time.reshape(-1, features), time_out_weights, preferred_element_type=jnp.float32
    ).reshape(after_space.shape)
    stab_index = lax.axis_index("stab") * stabs_here + jnp.arange(stabs_here)
    real_mask = (stab_index < STABS_REAL).astype(jnp.float32)
    grad_after = readout_grad(after_time, readout, labels, real_mask)
    grad_attended = contract(
        "td,ed->te", grad_after.astype(jnp.bfloat16).reshape(-1, features), time_out_weights
    )
    grad_attended = grad_attended.astype(jnp.bfloat16).reshape(attended_time.shape)
    spread = delta_rows(attended_time, grad_attended)
    queries_all, grad_all = (
        lax.all_gather(queries, "round", axis=0, tiled=True),
        lax.all_gather(grad_attended, "round", axis=0, tiled=True),
    )
    logsum_all, spread_all = (
        lax.all_gather(logsum_time, "round", axis=0, tiled=True),
        lax.all_gather(spread, "round", axis=0, tiled=True),
    )
    grad_queries = time_backward(
        queries, keys_all, values_all, grad_attended, logsum_time, spread, offset, 0
    )[0]
    grad_keys, grad_values = time_key_side(
        queries_all, key_rows, values, grad_all, logsum_all, spread_all, offset
    )
    grad_three = (
        grad_queries.astype(jnp.bfloat16),
        grad_keys.astype(jnp.bfloat16),
        grad_values.astype(jnp.bfloat16),
    )
    stacked = jnp.stack(grad_three).reshape(3, rounds_here, stabs_here, features)
    grad_normed = contract("crse,dce->rsd", stacked, time_three)
    grad_space = grad_after + norm_back(after_space, inverse_time, time_gain, grad_normed)
    grad_mixed = contract("rsd,hkd->rhsk", grad_space.astype(jnp.bfloat16), space_three).astype(
        jnp.bfloat16
    )
    grad_mixed = grad_mixed.reshape(rounds_here * HEADS, stabs_here, HEAD_DIM)
    grad_items = lax.all_to_all(grad_mixed, "stab", split_axis=0, concat_axis=1, tiled=True)
    revert = jax.vmap(space_backward, in_axes=(0, 0, 0, None, 0, 0, 0))
    item_grads = revert(
        query_space, key_space, value_space, neighbours, attended_space, grad_items, logsum_space
    )
    back_grads = (
        lax.all_to_all(
            item_grads[0].astype(jnp.bfloat16), "stab", split_axis=1, concat_axis=0, tiled=True
        ),
        lax.all_to_all(
            item_grads[1].astype(jnp.bfloat16), "stab", split_axis=1, concat_axis=0, tiled=True
        ),
        lax.all_to_all(
            item_grads[2].astype(jnp.bfloat16), "stab", split_axis=1, concat_axis=0, tiled=True
        ),
    )
    stacked_space = jnp.stack(back_grads).reshape(3, rounds_here, HEADS, stabs_here, HEAD_DIM)
    grad_normed_space = contract("crhsk,dchk->rsd", stacked_space, space_four)
    return grad_space + norm_back(widened, inverse, space_gain, grad_normed_space)


def solution(mesh):
    in_specs = (
        P("round", "stab", None),
        P("round", "stab"),
        P(),
        P(),
        P(),
        P(),
        P(),
        P(),
        P(),
        P(),
    )
    out_specs = P("round", "stab", None)
    return jax.shard_map(body, mesh=mesh, in_specs=in_specs, out_specs=out_specs, check_vma=False)
```

profile of v0, /device:TPU:0, one launch (start us, length us, event | category | flops | bytes accessed | tf_op | source)
XLA Modules:
  0.0 1826.6 jit_solution(4877300113412160326)
XLA Ops:
  14.0 20.6 %all_to_all.120 = bf16[64,112,64]{1,2,0:T(8,128)(2,1)} all-to-all(bf16[64,112,64]{1,2,0:T(8,128)(2,1)S(1)} %bitcast.244), channel_id=1, replica_groups=mesh['round'=4,'stab'=8] {'stab'}, dimensions={0} | all-to-all | bytes 1835008 | tf_op jit(solution)/shard_map/all_to_all | solution.py:192
  34.5 17.8 all_to_all.121
  52.3 4.4 all-to-all-start.2
  60.7 11.5 all-to-all-done.2
  72.2 2.8 copy.168
  75.0 14.7 gather_fusion.1
  89.7 22.0 %copy.169 = bf16[8,224,16,4,64]{4,3,2,1,0:T(4,128)(2,1)} copy(bf16[8,224,16,4,64]{4,0,3,2,1:T(8,128)(2,1)} %bitcast.217) | data formatting | bytes 29360128 | tf_op jit(solution)/shard_map/vmap()/gather | solution.py:34
  111.6 15.3 gather_fusion
  126.9 21.9 %copy.167 = bf16[8,224,16,4,64]{4,3,2,1,0:T(4,128)(2,1)} copy(bf16[8,224,16,4,64]{4,0,3,2,1:T(8,128)(2,1)} %bitcast.216) | data formatting | bytes 29360128 | tf_op jit(solution)/shard_map/vmap()/gather | solution.py:34
  148.8 20.9 %multiply_reduce_fusion.1 = (f32[8,224,4]{2,1,0:T(8,128)}, f32[8,224,4,64]{3,2,1,0:T(4,128)S(1)}) fusion(bf16[8,224,4,64]{3,2,1,0:T(4,128)(2,1)} %bitcast.220, bf16[8,224,64,64]{3,2,1,0:T(8,128)(2,1)} %bitcast.210), kind=kOutput, calls=%fused_computation.36 | convolution fusion | flops 59630592 | bytes 17461248 | tf_op jit(solution)/shard_map/vmap(nid,njd->nij)/dot_general | solution.py:17
  169.7 26.7 %exponential_reduce_fusion.1 = f32[8,224,4]{2,1,0:T(8,128)S(1)} fusion(f32[8,224,4,64]{3,2,1,0:T(4,128)S(1)} %get-tuple-element.14, f32[8,224,4]{2,1,0:T(8,128)} %get-tuple-element.13), kind=kLoop, calls=%fused_computation.13 | loop fusion | flops 1369088 | bytes 1892352 | tf_op jit(solution)/shard_map/vmap()/reduce_sum | solution.py:61
  196.6 14.6 convolution_convert_fusion.1
  211.2 2.7 copy.253
  216.0 4.3 all-to-all-start.3
  222.0 12.4 all-to-all-done.3
  234.4 3.3 reshape.288
  250.7 66.1 %all-gather.5.cloned.1.call-done = bf16[32,448,128]{2,1,0:T(8,128)(2,1)} async-done(((bf16[8,448,128]{2,1,0:T(8,128)(2,1)}), bf16[32,448,128]{2,1,0:T(8,128)(2,1)}) %all-gather.5.cloned.1.call-update) | async-done | bytes 3670032 | tf_op jit(solution)/shard_map/all_gather | solution.py:208
  316.8 6.5 copy.175
  323.2 9.0 copy.179
  332.2 56.9 %all-gather.7.cloned.1.call-done = bf16[32,448,128]{2,1,0:T(8,128)(2,1)} async-done(((bf16[8,448,128]{2,1,0:T(8,128)(2,1)}), bf16[32,448,128]{2,1,0:T(8,128)(2,1)}) %all-gather.7.cloned.1.call-update) | async-done | bytes 3670032 | tf_op jit(solution)/shard_map/all_gather | solution.py:207
  389.1 6.4 copy.176
  395.5 9.0 copy.178
  404.5 7.9 fusion.15
  412.4 12.5 exponential_reduce_fusion
  425.0 4.6 convert_bitcast_fusion.5
  433.6 4.9 dot_general.77
  448.0 4.9 reshape_reshape.4
  453.1 14.0 all_gather.21
  468.0 3.2 multiply_reduce_fusion
  471.4 11.1 convert_bitcast_fusion.4
  482.5 2.9 copy.185
  487.3 14.2 all_gather.23
  501.8 6.9 copy.186
  508.7 9.0 copy.196
  517.8 9.0 fusion.30
  526.8 10.2 all-gather.11.cloned.1.call-done
  537.0 6.4 copy.191
  543.4 8.9 copy.193
  552.4 6.1 convert_bitcast_fusion.2
  561.8 10.0 convert_bitcast_fusion.3
  571.9 2.7 copy.197
  574.6 5.5 convert_element_type.188
  580.1 3.6 multiply_reduce_fusion.3
  586.6 3.8 all-to-all-start.4
  592.6 3.6 copy.205
  596.1 9.7 all-to-all-done.4
  610.4 20.9 %multiply_convert_fusion = bf16[8,224,4,64]{3,2,1,0:T(4,128)(2,1)} fusion(f32[8,224,4,64]{3,2,1,0:T(4,128)} %copy-done.2, bf16[8,224,4,64]{3,2,1,0:T(4,128)(2,1)S(1)} %bitcast.228, bf16[8,224,64,64]{3,2,1,0:T(8,128)(2,1)} %bitcast.219, f32[8,224,4]{2,1,0:T(8,128)S(1)} %copy.207, f32[8,224,4]{2,1,0:T(8,128)} %copy-done.17), kind=kOutput, calls=%fused_computation.4 | convolution fusion | flops 61472768 | bytes 18407424 | tf_op jit(solution)/shard_map/vmap(nid,njd->nij)/dot_general | solution.py:17
  631.3 13.8 convolution_convert_fusion
  647.6 4.4 reshape.293
  651.9 4.6 all-to-all-start.5
  656.6 27.0 %fusion.75 = f32[8,224,64,64]{3,2,1,0:T(8,128)} fusion(bf16[8,224,4,64]{3,2,1,0:T(4,128)(2,1)S(1)} %bitcast.229, f32[8,224,4,64]{3,2,1,0:T(4,128)} %copy-done.2, f32[8,224,4]{2,1,0:T(8,128)S(1)} %copy-done.18), kind=kOutput, calls=%fused_computation.116 | convolution fusion | flops 60096512 | bytes 32141312 | tf_op jit(solution)/shard_map/vmap(nij,nid->njd)/dot_general | solution.py:17
  683.6 62.5 %copy.214 = f32[224,16,8,4,64]{4,2,3,1,0:T(8,128)} copy(f32[224,16,8,4,64]{4,3,1,0,2:T(4,128)} %bitcast.212) | data formatting | bytes 58720256 | tf_op jit(solution)/shard_map/vmap()/reshape | solution.py:40
  748.3 468.5 %scatter_fusion.1 = f32[8,224,4,64]{3,0,2,1:T(8,128)} fusion(f32[8,224,4,64]{3,0,2,1:T(8,128)} %broadcast.88.clone, s32[3584]{0:T(1024)S(1)} %copy-done.16, f32[3584,8,4,64]{3,1,2,0:T(8,128)} %bitcast.214), kind=kCustom, calls=%fused_computation.3 | custom fusion | flops 7340032 | bytes 88094720 | tf_op jit(solution)/shard_map/vmap()/scatter-add | solution.py:41
  1216.9 3.7 convert_element_type.204
  1220.6 4.5 reshape.289
  1225.1 4.2 all-to-all-start.7
  1229.3 22.3 %fusion.80 = f32[8,224,64,64]{3,2,1,0:T(8,128)} fusion(bf16[8,224,4,64]{3,2,1,0:T(4,128)(2,1)} %multiply_convert_fusion, bf16[8,224,4,64]{3,2,1,0:T(4,128)(2,1)S(1)} %bitcast.221), kind=kOutput, calls=%fused_computation.121 | convolution fusion | flops 58720256 | bytes 31195136 | tf_op jit(solution)/shard_map/vmap(nij,nid->njd)/dot_general | solution.py:17
  1251.6 62.5 %copy.211 = f32[224,16,8,4,64]{4,2,3,1,0:T(8,128)} copy(f32[224,16,8,4,64]{4,3,1,0,2:T(4,128)} %bitcast.215) | data formatting | bytes 58720256 | tf_op jit(solution)/shard_map/vmap()/reshape | solution.py:40
  1316.3 468.5 %scatter_fusion = f32[8,224,4,64]{3,0,2,1:T(8,128)} fusion(f32[8,224,4,64]{3,0,2,1:T(8,128)} %broadcast.88.clone.1, s32[3584]{0:T(1024)S(1)} %copy-done.16, f32[3584,8,4,64]{3,1,2,0:T(8,128)} %bitcast.213), kind=kCustom, calls=%fused_computation.2 | custom fusion | flops 7340032 | bytes 88094720 | tf_op jit(solution)/shard_map/vmap()/scatter-add | solution.py:41
  1789.4 4.5 all-to-all-start.6
  1793.9 3.3 reshape.294
  1802.1 5.9 all-to-all-done.6
  1808.0 3.3 reshape.292
  1813.2 4.2 fusion.26
  (161 shorter events, 78.1 us)
Async XLA Ops:
  6.5 233.0 %copy-start = (bf16[512,512]{1,0:T(8,128)(2,1)S(1)}, bf16[512,512]{1,0:T(8,128)(2,1)}, u32[]{:S(2)}) copy-start(bf16[512,512]{1,0:T(8,128)(2,1)} %param.14) | copy-start | bytes 1572868
  6.5 3.3 copy-start.5
  6.5 3.3 copy-start.39
  8.1 4.0 copy-start.31
  9.8 2.3 copy-start.26
  14.0 42.8 %copy-start.37 = (s32[224,16]{0,1:T(8,128)S(1)}, s32[224,16]{0,1:T(8,128)}, u32[]{:S(2)}) copy-start(s32[224,16]{0,1:T(8,128)} %param.12) | copy-start | bytes 43012
  52.3 19.9 %all-to-all-start.2 = ((bf16[64,112,64]{1,2,0:T(8,128)(2,1)}), bf16[64,112,64]{1,2,0:T(8,128)(2,1)}, u32[]{:S(2)}, u32[]{:S(2)}) async-start(bf16[64,112,64]{1,2,0:T(8,128)(2,1)} %bitcast.16), calls=%async_computation.2 | async-start | bytes 2097152 | tf_op jit(solution)/shard_map/all_to_all | solution.py:193
  57.0 1.7 copy-start.15
  169.7 26.9 %copy-start.2 = (f32[8,224,4,64]{3,2,1,0:T(4,128)}, f32[8,224,4,64]{3,2,1,0:T(4,128)S(1)}, u32[]{:S(2)}) copy-start(f32[8,224,4,64]{3,2,1,0:T(4,128)S(1)} %get-tuple-element.14) | copy-start | bytes 5505028
  169.7 26.7 %copy-start.7 = (f32[8,224,4]{2,1,0:T(8,128)S(1)}, f32[8,224,4]{2,1,0:T(8,128)}, u32[]{:S(2)}) copy-start(f32[8,224,4]{2,1,0:T(8,128)} %get-tuple-element.13) | copy-start | bytes 86020
  196.5 14.7 copy-start.17
  216.0 4.4 copy-start.25
  216.0 18.4 %all-to-all-start.3 = ((bf16[8,2,28672]{2,1,0:T(2,128)(2,1)}), bf16[8,2,28672]{2,1,0:T(2,128)(2,1)}, u32[]{:S(2)}, u32[]{:S(2)}) async-start(bf16[8,2,28672]{2,1,0:T(2,128)(2,1)} %reshape.287), calls=%async_computation.3 | async-start | bytes 1835008 | tf_op jit(solution)/shard_map/all_to_all | solution.py:197
  220.4 96.4 %all-gather.5.cloned.1.call-start = ((), (), s32[]{:S(2)}) async-start(), calls=%async_computation.8 | async-start | bytes 4587520 | tf_op jit(solution)/shard_map/all_gather | solution.py:208
  239.6 2.1 copy-start.27
  239.6 2.1 copy-start.41
  241.7 1.7 copy-start.11
  241.7 342.2 %copy-start.33 = (f32[8,112]{1,0:T(8,128)}, f32[8,112]{1,0:T(8,128)S(1)}, u32[]{:S(2)}) copy-start(f32[8,112]{1,0:T(8,128)S(1)} %add_rsqrt_fusion) | copy-start | bytes 10756
  245.1 144.0 %all-gather.7.cloned.1.call-start = ((), (), s32[]{:S(2)}) async-start(), calls=%async_computation.9 | async-start | bytes 4587520 | tf_op jit(solution)/shard_map/all_gather | solution.py:207
  246.7 255.2 %all-gather.9.cloned.1.call-start = ((), (), s32[]{:S(2)}) async-start(), calls=%async_computation.10 | async-start | bytes 4587520 | tf_op jit(solution)/shard_map/all_gather | solution.py:223
  248.2 288.8 %all-gather.11.cloned.1.call-start = ((), (), s32[]{:S(2)}) async-start(), calls=%async_computation.11 | async-start | bytes 4587520 | tf_op jit(solution)/shard_map/all_gather | solution.py:224
  412.4 12.6 copy-start.4
  425.0 4.7 copy-start.21
  429.7 1.3 copy-start.9
  430.9 7.5 copy-start.43
  433.6 7.3 copy-start.38
  440.9 142.9 %copy-start.29 = (f32[8,112]{1,0:T(8,128)}, f32[8,112]{1,0:T(8,128)S(1)}, u32[]{:S(2)}) copy-start(f32[8,112]{1,0:T(8,128)S(1)} %subtract_multiply_fusion) | copy-start | bytes 10756
  442.7 1.5 copy-start.20
  446.1 21.9 %copy-start.10 = (bf16[8,448,2,64]{3,0,2,1:T(8,128)(2,1)S(1)}, bf16[8,448,2,64]{3,0,2,1:T(8,128)(2,1)}, u32[]{:S(2)}) copy-start(bf16[8,448,2,64]{3,0,2,1:T(8,128)(2,1)} %copy-done.9) | copy-start | bytes 2752516
  448.0 4.9 copy-start.22
  508.7 9.1 copy-start.8
  543.4 8.9 copy-start.19
  571.9 8.3 copy-start.28
  574.6 5.5 copy-start.12
  583.8 2.8 copy-start.23
  583.8 0.6 copy-start.35
  586.6 3.8 copy-start.14
  586.6 19.2 %all-to-all-start.4 = ((bf16[64,112,64]{1,2,0:T(8,128)(2,1)}), bf16[64,112,64]{1,2,0:T(8,128)(2,1)S(1)}, u32[]{:S(2)}, u32[]{:S(2)}) async-start(bf16[64,112,64]{1,2,0:T(8,128)(2,1)} %bitcast.256), calls=%async_computation.4 | async-start | bytes 2097152 | tf_op jit(solution)/shard_map/all_to_all | solution.py:248
  647.6 9.0 copy-start.18
  651.9 573.2 %all-to-all-start.5 = ((bf16[8,2,28672]{2,1,0:T(2,128)(2,1)}), bf16[8,2,28672]{2,1,0:T(2,128)(2,1)}, u32[]{:S(2)}, u32[]{:S(2)}) async-start(bf16[8,2,28672]{2,1,0:T(2,128)(2,1)} %reshape.293), calls=%async_computation.5 | async-start | bytes 1835008 | tf_op jit(solution)/shard_map/all_to_all | solution.py:254
  746.1 2.3 copy-start.16
  1220.6 8.7 copy-start.3
  1225.1 564.3 %all-to-all-start.7 = ((bf16[8,2,28672]{2,1,0:T(2,128)(2,1)}), bf16[8,2,28672]{2,1,0:T(2,128)(2,1)S(1)}, u32[]{:S(2)}, u32[]{:S(2)}) async-start(bf16[8,2,28672]{2,1,0:T(2,128)(2,1)} %reshape.289), calls=%async_computation.7 | async-start | bytes 1835008 | tf_op jit(solution)/shard_map/all_to_all | solution.py:260
  1789.4 18.5 %all-to-all-start.6 = ((bf16[8,2,28672]{2,1,0:T(2,128)(2,1)}), bf16[8,2,28672]{2,1,0:T(2,128)(2,1)}, u32[]{:S(2)}, u32[]{:S(2)}) async-start(bf16[8,2,28672]{2,1,0:T(2,128)(2,1)} %reshape.291), calls=%async_computation.6 | async-start | bytes 1835008 | tf_op jit(solution)/shard_map/all_to_all | solution.py:257
  1802.0 11.1 copy-start.6
  1802.0 11.1 copy-start.40
  1813.1 4.3 copy-start.13
  1813.1 4.3 copy-start.24
  1813.1 4.3 copy-start.30
  1813.1 4.3 copy-start.32
  1813.2 4.3 copy-start.34
  1813.2 4.3 copy-start.36
  1813.2 4.3 copy-start.42
  1813.2 4.3 copy-start.44
  1817.4 2.4 copy-start.1
Sparse Core Ops, SparseCore 0:
  245.2 71.4 all-gather.4
  318.3 70.7 all-gather.6
  390.7 72.2 all-gather.8
  464.4 72.5 all-gather.10
where the time goes:
time: 1840 us; the launch traced here: 1830 us
  other arithmetic  994 us (54%)
  local copies, waits for them, and re-layouts  365 us (20%)
  matrix products  189 us (10%)
  waiting for transfers between devices  173 us (9%)
  blocking collectives  66.5 us (4%)
  starting transfers between devices  26 us (1%)
    scatter-add x2, other arithmetic, spread_rows(): jnp.zeros((block_count, BLOCK, depth), near_grad.dtype).at[neighbours]  937 us
    dot_general x19, matrix products, contract(): jnp.einsum(form, first_operand, second_operand, preferred_element_type=jn...  186 us
    reshape x2, local copies, waits for them, and re-layouts, spread_rows(): pieces = near_grad.reshape(block_count, neighbours.shape[1], BLOCK, depth)  125 us
    gather x4, local copies, waits for them, and re-layouts, block_rows_of(): return blocked[neighbours].reshape(neighbours.shape[0], -1, depth)  73.8 us
    all_gather x1, waiting for transfers between devices, body(): lax.all_gather(values, 'round', axis=0, tiled=True)  66.1 us
    all_gather x1, waiting for transfers between devices, body(): lax.all_gather(key_rows, 'round', axis=0, tiled=True)  56.9 us
  transfers between devices with their start and end apart: 10, of which 7 were waited for; matrix products, arithmetic and copies ran while one was open for 70% of the time, Pallas kernels for 0%

commit v1 on v0

v1 whole, which is shorter than its diff:
```python
import functools

import jax
import jax.numpy as jnp
from jax import lax
from jax.experimental import pallas as pl
from jax.experimental.pallas import tpu as pltpu
from jax.sharding import PartitionSpec as P

HEADS = 8
HEAD_DIM = 64
STABS_REAL = 840
BLOCK = 4
PAIR = 2 * HEAD_DIM
CHUNK = 128
GROUP = 128

EPSILON = 1e-06
MASKED_SCORE = -1e30
FACTOR = HEAD_DIM ** (-0.5)
VMEM_LIMIT = 50 * 1024 * 1024


def dot(first, second):
    return jnp.dot(first, second, preferred_element_type=jnp.float32)


def dot_nt(first, second):
    return lax.dot_general(
        first, second, (((1,), (1,)), ((), ())), preferred_element_type=jnp.float32
    )


def dot_tn(first, second):
    return lax.dot_general(
        first, second, (((0,), (0,)), ((), ())), preferred_element_type=jnp.float32
    )


def inverse_rms(hidden):
    return lax.rsqrt(jnp.mean(hidden * hidden, axis=-1, keepdims=True) + EPSILON)


def norm_back(hidden, inverse, gain, upstream):
    scaled = upstream * gain
    inner = jnp.mean(hidden * scaled, axis=-1, keepdims=True)
    return inverse * scaled - hidden * (inverse * inverse * inverse * inner)


def softmax_rows(scores):
    highest = jnp.max(scores, axis=-1, keepdims=True)
    weights = jnp.exp(scores - highest)
    total = jnp.sum(weights, axis=-1, keepdims=True)
    return (weights * (1.0 / total)).astype(jnp.bfloat16)


def space_forward_kernel(
    x_ref, near_ref, gain_ref, wq_ref, wk_ref, wv_ref, wo_ref,
    h_ref, q_ref, k_ref, v_ref, o_ref, p_ref,
    n_scr, bias_scr, acc_scr,
):
    step = pl.program_id(0)
    stabs = x_ref.shape[0]
    blocks, links = near_ref.shape

    @pl.when(step == 0)
    def _():
        x = x_ref[...].astype(jnp.float32)
        n_scr[...] = (x * inverse_rms(x) * gain_ref[...]).astype(jnp.bfloat16)
        acc_scr[...] = x
        lanes = lax.broadcasted_iota(jnp.int32, (blocks, blocks), 1)
        near = near_ref[...]
        listed = jnp.zeros((blocks, blocks), jnp.float32)
        for link in range(links):
            listed = jnp.where(lanes == near[:, link : link + 1], 1.0, listed)
        owner = lax.broadcasted_iota(jnp.int32, (stabs, blocks), 0) // BLOCK
        column = lax.broadcasted_iota(jnp.int32, (stabs, blocks), 1)
        widen = jnp.where(owner == column, 1.0, 0.0).astype(jnp.bfloat16)
        rows = dot(widen, listed.astype(jnp.bfloat16)).astype(jnp.bfloat16)
        bias_scr[...] = jnp.where(dot_nt(rows, widen) > 0.5, 0.0, MASKED_SCORE)

    n = n_scr[...]
    q_ref[...] = dot(n, wq_ref[...]).astype(jnp.bfloat16)
    k_ref[...] = dot(n, wk_ref[...]).astype(jnp.bfloat16)
    v_ref[...] = dot(n, wv_ref[...]).astype(jnp.bfloat16)
    for head in range(2):
        cols = slice(head * HEAD_DIM, (head + 1) * HEAD_DIM)
        keys = k_ref[:, cols]
        values = v_ref[:, cols]
        for start in range(0, stabs, CHUNK):
            rows = slice(start, start + CHUNK)
            scores = dot_nt(q_ref[rows, cols] * FACTOR, keys) + bias_scr[rows, :]
            weights = softmax_rows(scores)
            p_ref[head, rows, :] = weights
            o_ref[rows, cols] = dot(weights, values).astype(jnp.bfloat16)
    acc_scr[...] += dot(o_ref[...], wo_ref[...])

    @pl.when(step == pl.num_programs(0) - 1)
    def _():
        h_ref[...] = acc_scr[...].astype(jnp.bfloat16)


def space_backward_kernel(
    x_ref, gain_ref, g_ref, q_ref, k_ref, v_ref, o_ref, p_ref,
    wq_ref, wk_ref, wv_ref, wo_ref,
    out_ref,
    gn_scr, go_scr, gs_scr, dq_scr, dk_scr, dv_scr,
):
    step = pl.program_id(0)
    stabs = x_ref.shape[0]
    go = dot_nt(g_ref[...], wo_ref[...]).astype(jnp.bfloat16)
    go_scr[...] = go
    product = go.astype(jnp.float32) * o_ref[...].astype(jnp.float32)
    q_turned = q_ref[...].T
    go_turned = go.T
    for head in range(2):
        cols = slice(head * HEAD_DIM, (head + 1) * HEAD_DIM)
        keys = k_ref[:, cols]
        values = v_ref[:, cols]
        delta = jnp.sum(product[:, cols], axis=-1, keepdims=True)
        for start in range(0, stabs, CHUNK):
            rows = slice(start, start + CHUNK)
            grad_weights = dot_nt(go_scr[rows, cols], values)
            weights = p_ref[head, rows, :].astype(jnp.float32)
            grad_scores = (
                weights * ((grad_weights - delta[start : start + CHUNK]) * FACTOR)
            ).astype(jnp.bfloat16)
            gs_scr[rows, :] = grad_scores
            dq_scr[rows, cols] = dot(grad_scores, keys).astype(jnp.bfloat16)
        dk_scr[cols, :] = dot(q_turned[cols, :], gs_scr[...]).astype(jnp.bfloat16)
        dv_scr[cols, :] = dot(go_turned[cols, :], p_ref[head]).astype(jnp.bfloat16)
    part = (
        dot_nt(dq_scr[...], wq_ref[...])
        + dot_nt(dk_scr[...].T, wk_ref[...])
        + dot_nt(dv_scr[...].T, wv_ref[...])
    )

    @pl.when(step == 0)
    def _():
        gn_scr[...] = part

    @pl.when(step > 0)
    def _():
        gn_scr[...] += part

    @pl.when(step == pl.num_programs(0) - 1)
    def _():
        x = x_ref[...].astype(jnp.float32)
        back = norm_back(x, inverse_rms(x), gain_ref[...], gn_scr[...])
        out_ref[...] = (g_ref[...].astype(jnp.float32) + back).astype(jnp.bfloat16)


def time_kernel(
    width, h_ref, side_ref, gain_ref, readout_ref, win_ref, wout_ref,
    g_ref,
    qkv_scr, p_scr, o_scr, d_scr,
):
    tokens, features = h_ref.shape
    hidden = h_ref[...].astype(jnp.float32)
    inverse = inverse_rms(hidden)
    gain = gain_ref[...]
    normed = (hidden * inverse * gain).astype(jnp.bfloat16)
    qkv_scr[...] = dot(normed, win_ref[...]).astype(jnp.bfloat16)
    left = lax.broadcasted_iota(jnp.int32, (tokens, tokens), 0)
    right = lax.broadcasted_iota(jnp.int32, (tokens, tokens), 1)
    kept = ((left % width) == (right % width)) & (right <= left)
    bias = jnp.where(kept, 0.0, MASKED_SCORE)

    def part(index, head):
        start = index * features + head * HEAD_DIM
        return slice(start, start + HEAD_DIM)

    for head in range(HEADS):
        queries = qkv_scr[:, part(0, head)]
        weights = softmax_rows(dot_nt(queries * FACTOR, qkv_scr[:, part(1, head)]) + bias)
        p_scr[head] = weights
        o_scr[:, part(0, head)] = dot(weights, qkv_scr[:, part(2, head)]).astype(jnp.bfloat16)
    attended = o_scr[...]
    readout = readout_ref[...]
    after = hidden + dot(attended, wout_ref[...])
    logits = jnp.sum(after * readout, axis=-1, keepdims=True)
    side = side_ref[...]
    grad_after = ((jax.nn.sigmoid(logits) - side[:, 0:1]) * side[:, 1:2]) * readout
    grad_attended = dot_nt(grad_after.astype(jnp.bfloat16), wout_ref[...]).astype(jnp.bfloat16)
    product = grad_attended.astype(jnp.float32) * attended.astype(jnp.float32)
    for head in range(HEADS):
        cols = part(0, head)
        queries = qkv_scr[:, cols]
        keys = qkv_scr[:, part(1, head)]
        values = qkv_scr[:, part(2, head)]
        grad_rows = grad_attended[:, cols]
        delta = jnp.sum(product[:, cols], axis=-1, keepdims=True)
        weights = p_scr[head]
        grad_weights = dot_nt(grad_rows, values)
        grad_scores = (
            weights.astype(jnp.float32) * ((grad_weights - delta) * FACTOR)
        ).astype(jnp.bfloat16)
        d_scr[:, cols] = dot(grad_scores, keys).astype(jnp.bfloat16)
        d_scr[:, part(1, head)] = dot_tn(grad_scores, queries).astype(jnp.bfloat16)
        d_scr[:, part(2, head)] = dot_tn(weights, grad_rows).astype(jnp.bfloat16)
    grad_normed = dot_nt(d_scr[...], win_ref[...])
    g_ref[...] = (grad_after + norm_back(hidden, inverse, gain, grad_normed)).astype(jnp.bfloat16)


def whole(*shape):
    return pl.BlockSpec(shape, lambda step: (0,) * len(shape))


def weight_specs(features):
    pairs = features // PAIR
    return [
        pl.BlockSpec((features, PAIR), lambda step: (0, step)),
        pl.BlockSpec((features, PAIR), lambda step: (0, pairs + step)),
        pl.BlockSpec((features, PAIR), lambda step: (0, 2 * pairs + step)),
        pl.BlockSpec((PAIR, features), lambda step: (step, 0)),
    ]


def space_forward(x, neighbours, gain, w_in, w_out):
    stabs, features = x.shape
    pairs = features // PAIR
    column = pl.BlockSpec((stabs, PAIR), lambda step: (0, step))
    rows = jax.ShapeDtypeStruct((stabs, features), jnp.bfloat16)
    square = pl.BlockSpec((2, stabs, stabs), lambda step: (step, 0, 0))
    return pl.pallas_call(
        space_forward_kernel,
        grid=(pairs,),
        in_specs=[whole(stabs, features), whole(*neighbours.shape), whole(1, features)]
        + weight_specs(features),
        out_specs=[whole(stabs, features), column, column, column, column, square],
        out_shape=[
            rows, rows, rows, rows, rows,
            jax.ShapeDtypeStruct((2 * pairs, stabs, stabs), jnp.bfloat16),
        ],
        scratch_shapes=[
            pltpu.VMEM((stabs, features), jnp.bfloat16),
            pltpu.VMEM((stabs, stabs), jnp.float32),
            pltpu.VMEM((stabs, features), jnp.float32),
        ],
        compiler_params=pltpu.CompilerParams(vmem_limit_bytes=VMEM_LIMIT),
        name="space_forward",
    )(x, neighbours, gain, w_in, w_in, w_in, w_out)


def space_backward(x, gain, grad, saved, w_in, w_out):
    stabs, features = x.shape
    pairs = features // PAIR
    column = pl.BlockSpec((stabs, PAIR), lambda step: (0, step))
    square = pl.BlockSpec((2, stabs, stabs), lambda step: (step, 0, 0))
    return pl.pallas_call(
        space_backward_kernel,
        grid=(pairs,),
        in_specs=[whole(stabs, features), whole(1, features), whole(stabs, features)]
        + [column] * 4
        + [square]
        + weight_specs(features),
        out_specs=whole(stabs, features),
        out_shape=jax.ShapeDtypeStruct((stabs, features), jnp.bfloat16),
        scratch_shapes=[
            pltpu.VMEM((stabs, features), jnp.float32),
            pltpu.VMEM((stabs, PAIR), jnp.bfloat16),
            pltpu.VMEM((stabs, stabs), jnp.bfloat16),
            pltpu.VMEM((stabs, PAIR), jnp.bfloat16),
            pltpu.VMEM((PAIR, stabs), jnp.bfloat16),
            pltpu.VMEM((PAIR, stabs), jnp.bfloat16),
        ],
        compiler_params=pltpu.CompilerParams(vmem_limit_bytes=VMEM_LIMIT),
        name="space_backward",
    )(x, gain, grad, *saved, w_in, w_in, w_in, w_out)


def time_both(hidden, side, gain, readout, w_in, w_out, width, tokens):
    total, features = hidden.shape
    row = pl.BlockSpec((tokens, features), lambda step: (step, 0))
    return pl.pallas_call(
        functools.partial(time_kernel, width),
        grid=(total // tokens,),
        in_specs=[
            row,
            pl.BlockSpec((tokens, 2), lambda step: (step, 0)),
            whole(1, features),
            whole(1, features),
            whole(*w_in.shape),
            whole(*w_out.shape),
        ],
        out_specs=row,
        out_shape=jax.ShapeDtypeStruct((total, features), jnp.bfloat16),
        scratch_shapes=[
            pltpu.VMEM((tokens, 3 * features), jnp.bfloat16),
            pltpu.VMEM((HEADS, tokens, tokens), jnp.bfloat16),
            pltpu.VMEM((tokens, features), jnp.bfloat16),
            pltpu.VMEM((tokens, 3 * features), jnp.bfloat16),
        ],
        compiler_params=pltpu.CompilerParams(vmem_limit_bytes=VMEM_LIMIT),
        name="time_both",
    )(hidden, side, gain, readout, w_in, w_out)


def body(
    round_size,
    stab_size,
    inputs,
    labels,
    neighbours,
    space_in_weights,
    space_out_weights,
    space_gain,
    time_in_weights,
    time_out_weights,
    time_gain,
    readout,
):
    rounds_here, stabs_here, features = inputs.shape
    rounds = rounds_here * round_size
    stabs = stabs_here * stab_size
    copies = stab_size // rounds_here
    assert copies * rounds_here == stab_size
    padded = -(-stabs_here // round_size) * round_size
    part = padded // round_size
    direct = copies == 1 and padded == stabs_here
    both = ("round", "stab")
    space_gain, time_gain, readout = space_gain[None], time_gain[None], readout[None]

    def to_rounds(tokens):
        if copies > 1:
            tokens = jnp.repeat(tokens, copies, axis=0)
        return lax.all_to_all(tokens, "stab", split_axis=0, concat_axis=1, tiled=True)[0]

    def to_tokens(rows):
        moved = lax.all_to_all(rows[None], "stab", split_axis=1, concat_axis=0, tiled=True)
        return moved[::copies] if copies > 1 else moved

    def pad_stabs(tokens):
        return jnp.pad(tokens, ((0, 0), (0, padded - stabs_here), (0, 0)))

    def to_times(rows):
        if direct:
            return lax.all_to_all(
                rows.reshape(rounds, part, features), both, split_axis=0, concat_axis=0, tiled=True
            )
        tokens = pad_stabs(to_tokens(rows))
        return lax.all_to_all(tokens, "round", split_axis=1, concat_axis=0, tiled=True)

    def from_times(times):
        if direct:
            moved = lax.all_to_all(times, both, split_axis=0, concat_axis=0, tiled=True)
            return moved.reshape(stabs, features)
        tokens = lax.all_to_all(times, "round", split_axis=0, concat_axis=1, tiled=True)
        return to_rounds(tokens[:, :stabs_here])

    here_round, here_stab = lax.axis_index("round"), lax.axis_index("stab")
    if direct:
        first = (here_round * stab_size + here_stab) * part
    else:
        first = here_stab * stabs_here + here_round * part
    slot = jnp.arange(part) + (here_round * part if not direct else 0)
    real = first + jnp.arange(part) < STABS_REAL
    if not direct:
        real = real & (slot < stabs_here)
    labels_all = lax.all_gather(labels, both, axis=0, tiled=False)
    labels_all = labels_all.reshape(round_size, stab_size, rounds_here, stabs_here)
    labels_all = jnp.transpose(labels_all, (0, 2, 1, 3)).reshape(rounds, stabs)
    labels_all = jnp.pad(labels_all, ((0, 0), (0, padded)))
    targets = lax.dynamic_slice(labels_all, (0, first), (rounds, part)).astype(jnp.float32)
    side = jnp.stack([targets, jnp.broadcast_to(real.astype(jnp.float32), targets.shape)], axis=-1)

    width = max(1, GROUP // rounds)
    while part % width:
        width -= 1
    groups = part // width
    tokens = width * rounds

    def to_groups(times):
        depth = times.shape[-1]
        split = times.reshape(rounds, groups, width, depth)
        return jnp.transpose(split, (1, 0, 2, 3)).reshape(groups * tokens, depth)

    def from_groups(rows):
        split = rows.reshape(groups, rounds, width, features)
        return jnp.transpose(split, (1, 0, 2, 3)).reshape(rounds, part, features)

    x = to_rounds(inputs)
    after_space, *saved = space_forward(
        x, neighbours, space_gain, space_in_weights, space_out_weights
    )
    times = to_groups(to_times(after_space))
    grad_times = time_both(
        times, to_groups(side), time_gain, readout, time_in_weights, time_out_weights, width, tokens
    )
    grad_space = from_times(from_groups(grad_times))
    grad = space_backward(x, space_gain, grad_space, saved, space_in_weights, space_out_weights)
    return to_tokens(grad).astype(jnp.float32)


def solution(mesh):
    in_specs = (
        P("round", "stab", None),
        P("round", "stab"),
        P(),
        P(),
        P(),
        P(),
        P(),
        P(),
        P(),
        P(),
    )
    out_specs = P("round", "stab", None)
    sized = functools.partial(body, mesh.shape["round"], mesh.shape["stab"])
    return jax.shard_map(sized, mesh=mesh, in_specs=in_specs, out_specs=out_specs, check_vma=False)
```

time: 1840 us -> 247 us (0.13)
  other arithmetic: 994 us -> 6.34 us
  local copies, waits for them, and re-layouts: 365 us -> 13.3 us
  matrix products: 189 us -> 0 us
  waiting for transfers between devices: 173 us -> 13.9 us
  Pallas kernels: 0 us -> 104 us
  blocking collectives: 66.5 us -> 98.9 us
    scatter-add x2 -> x0, other arithmetic: 937 us -> none  [spread_rows(): jnp.zeros((block_count, BLOCK, depth), near_grad.dtype).at[neighbours]]
    dot_general x20 -> x0, matrix products: 189 us -> none  [the longest x19 186 us: contract(): jnp.einsum(form, first_operand, second_operand, preferred_element_type=jn...]
    reshape x8, local copies, waits for them, and re-layouts: 165 us -> 3.68 us  [the longest x1 1.29 us: from_times(): return moved.reshape(stabs, features)]
    all_gather x4 -> x0, waiting for transfers between devices: 133 us -> none  [the longest x1 66.1 us: body(): lax.all_gather(values, 'round', axis=0, tiled=True)]
    pallas_call x0 -> x3, Pallas kernels: none -> 104 us  [the longest x1 43.7 us: time_both(): pl.pallas_call(functools.partial(time_kernel, width), grid=(total // toke...]
    gather x4 -> x0, local copies, waits for them, and re-layouts: 73.8 us -> none  [block_rows_of(): return blocked[neighbours].reshape(neighbours.shape[0], -1, depth)]
    reduce_sum x5 -> x0, other arithmetic: 46 us -> none  [the longest x1 26.7 us: space_forward(): jnp.sum(jnp.exp(scores - highest), axis=-1, keepdims=True)]
    all_gather x4 -> x0, local copies, waits for them, and re-layouts: 26.2 us -> none  [the longest x1 6.89 us: body(): lax.all_gather(queries, 'round', axis=0, tiled=True)]
  transfers between devices with their start and end apart: 10 -> 2, of which waited for: 7 -> 1; matrix products, arithmetic and copies ran while one was open for 70% -> 0% of each run, Pallas kernels for 0% -> 0%
where the time goes in v1:
time: 247 us; the launch traced here: 246 us
  Pallas kernels  104 us (42%)
  blocking collectives  98.9 us (40%)
  waiting for transfers between devices  13.9 us (6%)
  local copies, waits for them, and re-layouts  13.3 us (5%)
  starting transfers between devices  9.32 us (4%)
  other arithmetic  6.34 us (3%)
    all_gather x1, blocking collectives, body(): labels_all = lax.all_gather(labels, both, axis=0, tiled=False)  52.7 us
    pallas_call x1, Pallas kernels, time_both(): pl.pallas_call(functools.partial(time_kernel, width), grid=(total // toke...  43.7 us
    pallas_call x1, Pallas kernels, space_forward(): pl.pallas_call(space_forward_kernel, grid=(pairs,), in_specs=[whole(stabs...  35.7 us
    all_to_all x1, blocking collectives, from_times(): moved = lax.all_to_all(times, both, split_axis=0, concat_axis=0, tiled=True)  28.8 us
    pallas_call x1, Pallas kernels, space_backward(): pl.pallas_call(space_backward_kernel, grid=(pairs,), in_specs=[whole(stab...  24.9 us
    all_to_all x1, blocking collectives, to_tokens(): lax.all_to_all(rows[None], 'stab', split_axis=1, concat_axis=0, tiled=True)  17.4 us
    all_to_all x1, waiting for transfers between devices, to_rounds(): lax.all_to_all(tokens, 'stab', split_axis=0, concat_axis=1, tiled=True)[0]  13.9 us
    unnamed x27, local copies, waits for them, and re-layouts  6.57 us
  transfers between devices with their start and end apart: 2, of which 1 were waited for; matrix products, arithmetic and copies ran while one was open for 0% of the time, Pallas kernels for 0%

profile of v1, /device:TPU:0, one launch (start us, length us, event | category | flops | bytes accessed | tf_op | source)
XLA Modules:
  0.0 246.2 jit_solution(16612793169611002103)
XLA Ops:
  0.0 0.0 copy-start.9
  0.0 0.0 copy-start.6
  0.0 0.0 copy-start.2
  0.0 5.3 %all-to-all-start = ((bf16[8,112,512]{2,1,0:T(8,128)(2,1)}), bf16[8,112,512]{2,1,0:T(8,128)(2,1)S(1)}, u32[]{:S(2)}, u32[]{:S(2)}) async-start(bf16[8,112,512]{2,1,0:T(8,128)(2,1)} %param.10), calls=%async_computation | async-start | bytes 1835008 | tf_op jit(solution)/shard_map/all_to_all | solution.py:327
  5.3 0.0 copy-done.9
  5.3 0.1 copy.21.near_ref
  5.4 13.9 %all-to-all-done = bf16[8,112,512]{2,1,0:T(8,128)(2,1)S(1)} async-done(((bf16[8,112,512]{2,1,0:T(8,128)(2,1)}), bf16[8,112,512]{2,1,0:T(8,128)(2,1)S(1)}, u32[]{:S(2)}, u32[]{:S(2)}) %all-to-all-start) | async-done | bytes 917536 | tf_op jit(solution)/shard_map/all_to_all | solution.py:327
  19.3 0.0 copy-start
  19.3 0.9 copy-done
  20.3 0.0 copy-done.6
  20.3 0.0 copy-done.2
  20.3 35.7 %space_forward.1 = (bf16[896,512]{1,0:T(8,128)(2,1)S(1)}, bf16[896,512]{1,0:T(8,128)(2,1)S(1)}, bf16[896,512]{1,0:T(8,128)(2,1)S(1)}, bf16[896,512]{1,0:T(8,128)...) custom-call(bf16[896,512]{1,0:T(8,128)(2,1)} %bitcast.27, s32[224,16]{1,0:T(8,128)S(1)} %copy.21.near_ref, ...), custom_call_target="tpu_custom_call" | custom-call | tf_op jit(solution)/shard_map/space_forward/pallas_call | solution.py:225
  55.9 0.0 copy-start.3
  55.9 0.9 copy-done.3
  56.9 0.0 copy-start.4
  56.9 1.0 copy-done.4
  57.8 0.0 copy-start.10
  57.8 1.1 reshape.42
  59.0 4.0 %all-to-all-start.1 = ((bf16[32,28,512]{2,1,0:T(8,128)(2,1)}), bf16[32,28,512]{2,1,0:T(8,128)(2,1)S(1)}, u32[]{:S(2)}, u32[]{:S(2)}) async-start(bf16[32,28,512]{2,1,0:T(8,128)(2,1)} %reshape.42), calls=%async_computation.1 | async-start | bytes 2097152 | tf_op jit(solution)/shard_map/all_to_all | solution.py:338
  63.0 0.0 copy-done.10
  63.0 52.7 %all-gather = s32[256,112]{1,0:T(8,128)S(1)} all-gather(s32[8,112]{1,0:T(8,128)S(1)} %copy-done.10), channel_id=2, replica_groups=mesh['round'=4,'stab'=8] {'round','stab'}, dimensions={0}, use_global_device_ids=true | all-gather | bytes 118272 | tf_op jit(solution)/shard_map/all_gather | solution.py:360
  115.7 0.1 reshape.46
  115.8 0.1 fusion
  115.9 0.1 copy.25
  116.0 0.1 stack_broadcast_in_dim.3
  116.1 0.3 copy.26
  116.4 0.0 all-to-all-done.1
  116.4 0.5 copy.22
  116.9 0.0 copy-start.5
  116.9 0.0 copy-start.7
  116.9 0.0 copy-start.8
  117.0 0.7 copy.23
  117.7 0.2 reshape.44.h_ref
  117.9 0.1 copy-done.5
  118.0 0.0 copy-done.7
  118.0 0.0 copy-done.8
  118.0 43.7 %time_both.1 = bf16[896,512]{1,0:T(8,128)(2,1)S(1)} custom-call(bf16[896,512]{1,0:T(8,128)(2,1)S(1)} %reshape.44.h_ref, f32[896,2]{1,0:T(8,128)S(1)} %bitcast.30, f32[1,512]{1,0:T(1,128)S(1)} %bitcast.33, f32[1,512]{1,0:T(1,128)S(1)} %bitcast.34, bf16[512,1536]{1,0:T(8,128)(2,1)} %win_ref.1, bf16[512,512]{1,0:T(8,128)(2,1)S(1)} %copy-done.5), custom_call_target="tpu_custom_call" | custom-call | tf_op jit(solution)/shard_map/time_both/pallas_call | solution.py:275
  161.6 0.2 reshape.48
  161.9 0.2 copy.27
  162.1 0.5 copy.28
  162.6 0.0 copy-start.1
  162.6 28.8 %all_to_all.28 = bf16[32,28,512]{2,1,0:T(8,128)(2,1)} all-to-all(bf16[32,28,512]{2,1,0:T(8,128)(2,1)S(1)} %copy.28), channel_id=1, replica_groups=mesh['round'=4,'stab'=8] {'round','stab'}, dimensions={0} | all-to-all | bytes 1835008 | tf_op jit(solution)/shard_map/all_to_all | solution.py:346
  191.3 1.3 reshape.50.g_ref
  192.6 0.0 copy-done.1
  192.7 24.9 %space_backward.1 = bf16[896,512]{1,0:T(8,128)(2,1)S(1)} custom-call(bf16[896,512]{1,0:T(8,128)(2,1)S(1)} %bitcast.28, f32[1,512]{1,0:T(1,128)S(1)} %bitcast.32, bf16[896,512]{1,0:T(8,128)(2,1)S(1)} %reshape.50.g_ref, bf16[896,512]{1,0:T(8,128)(2,1)} %copy-done.3, bf16[896,512]{1,0:T(8,128)(2,1)} %copy-done.4, bf16[896,512]{1,0:T(8,128)(2,1)} %get-tuple-element.14.v_ref, ...), custom_call_target="tpu_custom_call" | custom-call | tf_op jit(solution)/shard_map/space_backward/pallas_call | solution.py:250
  217.5 1.4 copy.34
  219.0 0.5 broadcast.12
  219.5 6.2 %reduce = bf16[896,512]{1,0:T(8,128)(2,1)S(1)} reduce(bf16[896,1,512]{2,1,0:T(2,128)(2,1)S(1)} %bitcast.36, bf16[]{:T(256)} %broadcast.12), dimensions={1}, to_apply=%bitcast.26.reduce_sub_computation | reduce | bytes 1835010
  225.7 0.7 reshape.54
  226.4 17.4 %all_to_all.29 = bf16[8,2,28672]{2,1,0:T(2,128)(2,1)S(1)} all-to-all(bf16[8,2,28672]{2,1,0:T(2,128)(2,1)S(1)} %reshape.54), channel_id=1, replica_groups=mesh['round'=4,'stab'=8] {'stab'}, dimensions={0} | all-to-all | bytes 1835008 | tf_op jit(solution)/shard_map/all_to_all | solution.py:330
  243.8 0.9 reshape.55
  244.8 1.4 copy.30
  (4 shorter events, 0.1 us)
Async XLA Ops:
  0.0 5.3 %copy-start.9 = (s32[224,16]{0,1:T(8,128)S(1)}, s32[224,16]{0,1:T(8,128)}, u32[]{:S(2)}) copy-start(s32[224,16]{0,1:T(8,128)} %param.12) | copy-start | bytes 43012
  0.0 20.3 %copy-start.6 = (f32[512]{0:T(512)S(1)}, f32[512]{0:T(512)}, u32[]{:S(2)}) copy-start(f32[512]{0:T(512)} %param.15) | copy-start | bytes 6148
  0.0 20.3 %copy-start.2 = (bf16[512,512]{1,0:T(8,128)(2,1)S(1)}, bf16[512,512]{1,0:T(8,128)(2,1)}, u32[]{:S(2)}) copy-start(bf16[512,512]{1,0:T(8,128)(2,1)} %wo_ref.3) | copy-start | bytes 1572868
  0.0 19.3 %all-to-all-start = ((bf16[8,112,512]{2,1,0:T(8,128)(2,1)}), bf16[8,112,512]{2,1,0:T(8,128)(2,1)S(1)}, u32[]{:S(2)}, u32[]{:S(2)}) async-start(bf16[8,112,512]{2,1,0:T(8,128)(2,1)} %param.10), calls=%async_computation | async-start | bytes 1835008 | tf_op jit(solution)/shard_map/all_to_all | solution.py:327
  19.3 0.9 copy-start
  55.9 0.9 copy-start.3
  56.9 1.0 copy-start.4
  57.8 5.2 %copy-start.10 = (s32[8,112]{1,0:T(8,128)S(1)}, s32[8,112]{1,0:T(8,128)}, u32[]{:S(2)}) copy-start(s32[8,112]{1,0:T(8,128)} %param.11) | copy-start | bytes 10756
  59.0 57.4 %all-to-all-start.1 = ((bf16[32,28,512]{2,1,0:T(8,128)(2,1)}), bf16[32,28,512]{2,1,0:T(8,128)(2,1)S(1)}, u32[]{:S(2)}, u32[]{:S(2)}) async-start(bf16[32,28,512]{2,1,0:T(8,128)(2,1)} %reshape.42), calls=%async_computation.1 | async-start | bytes 2097152 | tf_op jit(solution)/shard_map/all_to_all | solution.py:338
  116.9 1.0 copy-start.5
  116.9 1.0 copy-start.7
  116.9 1.0 copy-start.8
  162.6 30.1 %copy-start.1 = (bf16[8,112,512]{2,1,0:T(8,128)(2,1)S(1)}, bf16[8,112,512]{2,1,0:T(8,128)(2,1)}, u32[]{:S(2)}) copy-start(bf16[8,112,512]{2,1,0:T(8,128)(2,1)} %copy-done) | copy-start | bytes 2752516

commit v2 on v1

--- a/solution.py
+++ b/solution.py
@@ -12,7 +12,8 @@
 STABS_REAL = 840
 BLOCK = 4
 PAIR = 2 * HEAD_DIM
-CHUNK = 128
+CHUNK = 448
+BACK_CHUNK = 448
 GROUP = 128
 
 EPSILON = 1e-06
@@ -118,12 +119,12 @@
         keys = k_ref[:, cols]
         values = v_ref[:, cols]
         delta = jnp.sum(product[:, cols], axis=-1, keepdims=True)
-        for start in range(0, stabs, CHUNK):
-            rows = slice(start, start + CHUNK)
+        for start in range(0, stabs, BACK_CHUNK):
+            rows = slice(start, start + BACK_CHUNK)
             grad_weights = dot_nt(go_scr[rows, cols], values)
             weights = p_ref[head, rows, :].astype(jnp.float32)
             grad_scores = (
-                weights * ((grad_weights - delta[start : start + CHUNK]) * FACTOR)
+                weights * ((grad_weights - delta[start : start + BACK_CHUNK]) * FACTOR)
             ).astype(jnp.bfloat16)
             gs_scr[rows, :] = grad_scores
             dq_scr[rows, cols] = dot(grad_scores, keys).astype(jnp.bfloat16)
@@ -153,9 +154,11 @@
 def time_kernel(
     width, h_ref, side_ref, gain_ref, readout_ref, win_ref, wout_ref,
     g_ref,
-    qkv_scr, p_scr, o_scr, d_scr,
+    qkv_scr, p_scr, o_scr, go_scr, d_scr,
 ):
-    tokens, features = h_ref.shape
+    total, features = h_ref.shape
+    tokens = p_scr.shape[-1]
+    groups = total // tokens
     hidden = h_ref[...].astype(jnp.float32)
     inverse = inverse_rms(hidden)
     gain = gain_ref[...]
@@ -165,41 +168,83 @@
     right = lax.broadcasted_iota(jnp.int32, (tokens, tokens), 1)
     kept = ((left % width) == (right % width)) & (right <= left)
     bias = jnp.where(kept, 0.0, MASKED_SCORE)
-
-    def part(index, head):
-        start = index * features + head * HEAD_DIM
-        return slice(start, start + HEAD_DIM)
-
-    for head in range(HEADS):
-        queries = qkv_scr[:, part(0, head)]
-        weights = softmax_rows(dot_nt(queries * FACTOR, qkv_scr[:, part(1, head)]) + bias)
-        p_scr[head] = weights
-        o_scr[:, part(0, head)] = dot(weights, qkv_scr[:, part(2, head)]).astype(jnp.bfloat16)
-    attended = o_scr[...]
+    bias = jnp.concatenate([bias, bias], axis=0)
+
+    pairs = features // PAIR
+    lanes = lax.broadcasted_iota(jnp.int32, (tokens, PAIR), 1)
+    near = lanes < HEAD_DIM
+
+    def part(index, pair):
+        start = index * features + pair * PAIR
+        return slice(start, start + PAIR)
+
+    def rows_of(group):
+        return pl.ds(pl.multiple_of(group * tokens, tokens), tokens)
+
+    def stacked(block):
+        empty = jnp.zeros_like(block)
+        return jnp.concatenate(
+            [jnp.where(near, block, empty), jnp.where(near, empty, block)], axis=0
+        )
+
+    def merged(block):
+        return jnp.where(near, block[:tokens], block[tokens:]).astype(jnp.bfloat16)
+
+    def ahead(group, carry):
+        rows = rows_of(group)
+        scores = [
+            dot_nt(stacked(qkv_scr[rows, part(0, pair)] * FACTOR), qkv_scr[rows, part(1, pair)])
+            for pair in range(pairs)
+        ]
+        weights = [softmax_rows(score + bias) for score in scores]
+        for pair in range(pairs):
+            p_scr[group * pairs + pair] = weights[pair]
+        outs = [dot(weights[pair], qkv_scr[rows, part(2, pair)]) for pair in range(pairs)]
+        for pair in range(pairs):
+            o_scr[rows, part(0, pair)] = merged(outs[pair])
+        return carry
+
+    lax.fori_loop(0, groups, ahead, 0)
     readout = readout_ref[...]
-    after = hidden + dot(attended, wout_ref[...])
+    after = hidden + dot(o_scr[...], wout_ref[...])
     logits = jnp.sum(after * readout, axis=-1, keepdims=True)
     side = side_ref[...]
-    grad_after = ((jax.nn.sigmoid(logits) - side[:, 0:1]) * side[:, 1:2]) * readout
-    grad_attended = dot_nt(grad_after.astype(jnp.bfloat16), wout_ref[...]).astype(jnp.bfloat16)
-    product = grad_attended.astype(jnp.float32) * attended.astype(jnp.float32)
-    for head in range(HEADS):
-        cols = part(0, head)
-        queries = qkv_scr[:, cols]
-        keys = qkv_scr[:, part(1, head)]
-        values = qkv_scr[:, part(2, head)]
-        grad_rows = grad_attended[:, cols]
-        delta = jnp.sum(product[:, cols], axis=-1, keepdims=True)
-        weights = p_scr[head]
-        grad_weights = dot_nt(grad_rows, values)
-        grad_scores = (
-            weights.astype(jnp.float32) * ((grad_weights - delta) * FACTOR)
-        ).astype(jnp.bfloat16)
-        d_scr[:, cols] = dot(grad_scores, keys).astype(jnp.bfloat16)
-        d_scr[:, part(1, head)] = dot_tn(grad_scores, queries).astype(jnp.bfloat16)
-        d_scr[:, part(2, head)] = dot_tn(weights, grad_rows).astype(jnp.bfloat16)
+    grad_logits = (jax.nn.sigmoid(logits) - side[:, 0:1]) * side[:, 1:2]
+    grad_after = grad_logits * readout
+    go_scr[...] = dot_nt(grad_after.astype(jnp.bfloat16), wout_ref[...]).astype(jnp.bfloat16)
+
+    def behind(group, carry):
+        rows = rows_of(group)
+        span = range(pairs)
+        upstream = [stacked(go_scr[rows, part(0, pair)]) for pair in span]
+        products = [dot_nt(upstream[pair], qkv_scr[rows, part(2, pair)]) for pair in span]
+        weights = [p_scr[group * pairs + pair] for pair in span]
+        grad_scores = []
+        for pair in span:
+            attended = o_scr[rows, part(0, pair)].astype(jnp.float32)
+            attended = jnp.concatenate([attended, attended], axis=0)
+            delta = jnp.sum(
+                upstream[pair].astype(jnp.float32) * attended, axis=-1, keepdims=True
+            )
+            grad_scores.append(
+                (weights[pair].astype(jnp.float32) * ((products[pair] - delta) * FACTOR)).astype(
+                    jnp.bfloat16
+                )
+            )
+        queries = [dot(grad_scores[pair], qkv_scr[rows, part(1, pair)]) for pair in span]
+        keys = [dot_tn(grad_scores[pair], stacked(qkv_scr[rows, part(0, pair)])) for pair in span]
+        values = [dot_tn(weights[pair], upstream[pair]) for pair in span]
+        for pair in span:
+            d_scr[rows, part(0, pair)] = merged(queries[pair])
+            d_scr[rows, part(1, pair)] = keys[pair].astype(jnp.bfloat16)
+            d_scr[rows, part(2, pair)] = values[pair].astype(jnp.bfloat16)
+        return carry
+
+    lax.fori_loop(0, groups, behind, 0)
     grad_normed = dot_nt(d_scr[...], win_ref[...])
-    g_ref[...] = (grad_after + norm_back(hidden, inverse, gain, grad_normed)).astype(jnp.bfloat16)
+    hidden = h_ref[...].astype(jnp.float32)
+    back = norm_back(hidden, inverse, gain, grad_normed)
+    g_ref[...] = (grad_logits * readout + back).astype(jnp.bfloat16)
 
 
 def whole(*shape):
@@ -271,25 +316,15 @@
 
 def time_both(hidden, side, gain, readout, w_in, w_out, width, tokens):
     total, features = hidden.shape
-    row = pl.BlockSpec((tokens, features), lambda step: (step, 0))
     return pl.pallas_call(
         functools.partial(time_kernel, width),
-        grid=(total // tokens,),
-        in_specs=[
-            row,
-            pl.BlockSpec((tokens, 2), lambda step: (step, 0)),
-            whole(1, features),
-            whole(1, features),
-            whole(*w_in.shape),
-            whole(*w_out.shape),
-        ],
-        out_specs=row,
         out_shape=jax.ShapeDtypeStruct((total, features), jnp.bfloat16),
         scratch_shapes=[
-            pltpu.VMEM((tokens, 3 * features), jnp.bfloat16),
-            pltpu.VMEM((HEADS, tokens, tokens), jnp.bfloat16),
-            pltpu.VMEM((tokens, features), jnp.bfloat16),
-            pltpu.VMEM((tokens, 3 * features), jnp.bfloat16),
+            pltpu.VMEM((total, 3 * features), jnp.bfloat16),
+            pltpu.VMEM((total // tokens * (features // PAIR), 2 * tokens, tokens), jnp.bfloat16),
+            pltpu.VMEM((total, features), jnp.bfloat16),
+            pltpu.VMEM((total, features), jnp.bfloat16),
+            pltpu.VMEM((total, 3 * features), jnp.bfloat16),
         ],
         compiler_params=pltpu.CompilerParams(vmem_limit_bytes=VMEM_LIMIT),
         name="time_both",
@@ -327,7 +362,8 @@
         return lax.all_to_all(tokens, "stab", split_axis=0, concat_axis=1, tiled=True)[0]
 
     def to_tokens(rows):
-        moved = lax.all_to_all(rows[None], "stab", split_axis=1, concat_axis=0, tiled=True)
+        split = rows.reshape(stab_size, stabs_here, features)
+        moved = lax.all_to_all(split, "stab", split_axis=0, concat_axis=0, tiled=True)
         return moved[::copies] if copies > 1 else moved
 
     def pad_stabs(tokens):
@@ -351,17 +387,24 @@
     here_round, here_stab = lax.axis_index("round"), lax.axis_index("stab")
     if direct:
         first = (here_round * stab_size + here_stab) * part
+        chunks = jnp.transpose(labels.reshape(rounds_here, round_size, part), (1, 0, 2))
+        sent = jnp.tile(chunks.reshape(round_size, rounds_here * part), (stab_size, 1))
+        came = lax.all_to_all(sent, both, split_axis=0, concat_axis=0, tiled=True)
+        came = came.reshape(round_size, stab_size, rounds_here, part)
+        owner = (here_round * stab_size + here_stab) // round_size
+        targets = lax.dynamic_index_in_dim(came, owner, 1, keepdims=False)
+        targets = targets.reshape(rounds, part).astype(jnp.float32)
     else:
         first = here_stab * stabs_here + here_round * part
+        labels_all = lax.all_gather(labels, both, axis=0, tiled=False)
+        labels_all = labels_all.reshape(round_size, stab_size, rounds_here, stabs_here)
+        labels_all = jnp.transpose(labels_all, (0, 2, 1, 3)).reshape(rounds, stabs)
+        labels_all = jnp.pad(labels_all, ((0, 0), (0, padded)))
+        targets = lax.dynamic_slice(labels_all, (0, first), (rounds, part)).astype(jnp.float32)
     slot = jnp.arange(part) + (here_round * part if not direct else 0)
     real = first + jnp.arange(part) < STABS_REAL
     if not direct:
         real = real & (slot < stabs_here)
-    labels_all = lax.all_gather(labels, both, axis=0, tiled=False)
-    labels_all = labels_all.reshape(round_size, stab_size, rounds_here, stabs_here)
-    labels_all = jnp.transpose(labels_all, (0, 2, 1, 3)).reshape(rounds, stabs)
-    labels_all = jnp.pad(labels_all, ((0, 0), (0, padded)))
-    targets = lax.dynamic_slice(labels_all, (0, first), (rounds, part)).astype(jnp.float32)
     side = jnp.stack([targets, jnp.broadcast_to(real.astype(jnp.float32), targets.shape)], axis=-1)
 
     width = max(1, GROUP // rounds)

time: 247 us -> 174 us (0.70)
  blocking collectives: 98.9 us -> 47.1 us
  Pallas kernels: 104 us -> 64.1 us
  waiting for transfers between devices: 13.9 us -> 38.4 us
  local copies, waits for them, and re-layouts: 13.3 us -> 7.24 us
  starting transfers between devices: 9.32 us -> 15.3 us
  other arithmetic: 6.34 us -> 1.59 us
    all_gather x1 -> x0, blocking collectives: 52.7 us -> none  [body(): labels_all = lax.all_gather(labels, both, axis=0, tiled=False)]
    pallas_call x1, Pallas kernels: 43.7 us -> 15.9 us  [time_both(): pl.pallas_call(functools.partial(time_kernel, width), out_shape=jax.Shape...]
    all_to_all x1, waiting for transfers between devices: 0.01 us -> 25.2 us  [to_times(): lax.all_to_all(rows.reshape(rounds, part, features), both, split_axis=0,...]
    pallas_call x1, Pallas kernels: 35.7 us -> 26.7 us  [space_forward(): pl.pallas_call(space_forward_kernel, grid=(pairs,), in_specs=[whole(stabs...]
    unnamed x1 -> x0, other arithmetic: 6.24 us -> none
    unnamed x27 -> x23, local copies, waits for them, and re-layouts: 6.57 us -> 2.11 us
    all_to_all x0 -> x1, starting transfers between devices: none -> 4 us  [body(): came = lax.all_to_all(sent, both, split_axis=0, concat_axis=0, tiled=True)]
    pallas_call x1, Pallas kernels: 24.9 us -> 21.5 us  [space_backward(): pl.pallas_call(space_backward_kernel, grid=(pairs,), in_specs=[whole(stab...]
  transfers between devices with their start and end apart: 2 -> 3, of which waited for: 1 -> 2; matrix products, arithmetic and copies ran while one was open for 0% -> 1% of each run, Pallas kernels for 0% -> 15%
where the time goes in v2:
time: 174 us
  Pallas kernels  64.1 us (37%)
  blocking collectives  47.1 us (27%)
  waiting for transfers between devices  38.4 us (22%)
  starting transfers between devices  15.3 us (9%)
  local copies, waits for them, and re-layouts  7.24 us (4%)
    all_to_all x1, blocking collectives, from_times(): moved = lax.all_to_all(times, both, split_axis=0, concat_axis=0, tiled=True)  29.7 us
    pallas_call x1, Pallas kernels, space_forward(): pl.pallas_call(space_forward_kernel, grid=(pairs,), in_specs=[whole(stabs...  26.7 us
    all_to_all x1, waiting for transfers between devices, to_times(): lax.all_to_all(rows.reshape(rounds, part, features), both, split_axis=0,...  25.2 us
    pallas_call x1, Pallas kernels, space_backward(): pl.pallas_call(space_backward_kernel, grid=(pairs,), in_specs=[whole(stab...  21.5 us
    all_to_all x1, blocking collectives, to_tokens(): lax.all_to_all(split, 'stab', split_axis=0, concat_axis=0, tiled=True)  17.4 us
    pallas_call x1, Pallas kernels, time_both(): pl.pallas_call(functools.partial(time_kernel, width), out_shape=jax.Shape...  15.9 us
    all_to_all x1, waiting for transfers between devices, to_rounds(): lax.all_to_all(tokens, 'stab', split_axis=0, concat_axis=1, tiled=True)[0]  13.2 us
    all_to_all x1, starting transfers between devices, to_times(): lax.all_to_all(rows.reshape(rounds, part, features), both, split_axis=0,...  6.01 us
  transfers between devices with their start and end apart: 3, of which 2 were waited for; matrix products, arithmetic and copies ran while one was open for 1% of the time, Pallas kernels for 15%

profile of v2, /device:TPU:0, one launch (start us, length us, event | category | flops | bytes accessed | tf_op | source)
XLA Modules:
  0.0 174.0 jit_solution(15000942538377210499)
XLA Ops:
  0.0 0.0 copy-start.10
  0.0 0.0 copy-start.9
  0.0 0.0 copy-start.6
  0.0 0.0 copy-start.2
  0.0 5.3 %all-to-all-start = ((bf16[8,112,512]{2,1,0:T(8,128)(2,1)}), bf16[8,112,512]{2,1,0:T(8,128)(2,1)S(1)}, u32[]{:S(2)}, u32[]{:S(2)}) async-start(bf16[8,112,512]{2,1,0:T(8,128)(2,1)} %param.10), calls=%async_computation | async-start | bytes 1835008 | tf_op jit(solution)/shard_map/all_to_all | solution.py:362
  5.3 0.0 copy-done.10
  5.3 0.1 reshape.64
  5.4 0.1 tile.8
  5.5 0.6 all_to_all.24
  6.2 13.2 %all-to-all-done = bf16[8,112,512]{2,1,0:T(8,128)(2,1)S(1)} async-done(((bf16[8,112,512]{2,1,0:T(8,128)(2,1)}), bf16[8,112,512]{2,1,0:T(8,128)(2,1)S(1)}, u32[]{:S(2)}, u32[]{:S(2)}) %all-to-all-start) | async-done | bytes 917536 | tf_op jit(solution)/shard_map/all_to_all | solution.py:362
  19.3 0.0 copy-start
  19.3 4.0 %all-to-all-start.2 = ((s32[32,1,224]{2,1,0:T(1,128)}), s32[32,1,224]{2,1,0:T(1,128)S(1)}, u32[]{:S(2)}, u32[]{:S(2)}) async-start(s32[32,1,224]{2,1,0:T(1,128)} %all_to_all.24), calls=%async_computation.2 | async-start | bytes 65536 | tf_op jit(solution)/shard_map/all_to_all | solution.py:392
  23.4 0.0 copy-done.9
  23.4 0.1 copy.28.near_ref
  23.5 0.0 copy-done
  23.5 0.0 copy-done.6
  23.5 0.0 copy-done.2
  23.5 26.7 %space_forward.1 = (bf16[896,512]{1,0:T(8,128)(2,1)S(1)}, bf16[896,512]{1,0:T(8,128)(2,1)S(1)}, bf16[896,512]{1,0:T(8,128)(2,1)S(1)}, bf16[896,512]{1,0:T(8,128)...) custom-call(bf16[896,512]{1,0:T(8,128)(2,1)} %bitcast.19, s32[224,16]{1,0:T(8,128)S(1)} %copy.28.near_ref, ...), custom_call_target="tpu_custom_call" | custom-call | tf_op jit(solution)/shard_map/space_forward/pallas_call | solution.py:270
  50.2 0.0 copy-start.3
  50.2 1.0 copy-done.3
  51.2 0.0 copy-start.4
  51.2 0.9 copy-done.4
  52.1 1.1 reshape.61
  53.2 0.0 all-to-all-done.2
  53.2 6.0 %all-to-all-start.1 = ((bf16[32,28,512]{2,1,0:T(8,128)(2,1)}), bf16[32,28,512]{2,1,0:T(8,128)(2,1)S(1)}, u32[]{:S(2)}, u32[]{:S(2)}) async-start(bf16[32,28,512]{2,1,0:T(8,128)(2,1)} %reshape.61), calls=%async_computation.1 | async-start | bytes 2097152 | tf_op jit(solution)/shard_map/all_to_all | solution.py:374
  59.3 0.1 reduce
  59.4 0.1 reshape.65
  59.5 0.1 copy.32
  59.6 0.1 convert_element_type.22
  59.7 0.1 stack_broadcast_in_dim.3
  59.8 0.3 copy.33
  60.1 25.2 %all-to-all-done.1 = bf16[32,28,512]{2,1,0:T(8,128)(2,1)S(1)} async-done(((bf16[32,28,512]{2,1,0:T(8,128)(2,1)}), bf16[32,28,512]{2,1,0:T(8,128)(2,1)S(1)}, u32[]{:S(2)}, u32[]{:S(2)}) %all-to-all-start.1) | async-done | bytes 917536 | tf_op jit(solution)/shard_map/all_to_all | solution.py:374
  85.3 0.5 copy.29
  85.8 0.0 copy-start.5
  85.8 0.0 copy-start.7
  85.9 0.0 copy-start.8
  85.9 0.7 copy.30
  86.6 0.2 reshape.63.h_ref
  86.8 0.1 copy-done.5
  86.9 0.0 copy-done.7
  86.9 0.0 copy-done.8
  86.9 15.9 %time_both.1 = bf16[896,512]{1,0:T(8,128)(2,1)S(1)} custom-call(bf16[896,512]{1,0:T(8,128)(2,1)S(1)} %reshape.63.h_ref, f32[896,2]{1,0:T(8,128)S(1)} %bitcast.22, f32[1,512]{1,0:T(1,128)S(1)} %bitcast.25, f32[1,512]{1,0:T(1,128)S(1)} %bitcast.26, bf16[512,1536]{1,0:T(8,128)(2,1)} %win_ref.1, bf16[512,512]{1,0:T(8,128)(2,1)S(1)} %copy-done.5), custom_call_target="tpu_custom_call" | custom-call | tf_op jit(solution)/shard_map/time_both/pallas_call | solution.py:319
  102.8 0.2 reshape.67
  103.0 0.2 copy.34
  103.2 0.5 copy.35
  103.7 0.0 copy-start.1
  103.7 29.7 %all_to_all.33 = bf16[32,28,512]{2,1,0:T(8,128)(2,1)S(1)} all-to-all(bf16[32,28,512]{2,1,0:T(8,128)(2,1)S(1)} %copy.35), channel_id=1, replica_groups=mesh['round'=4,'stab'=8] {'round','stab'}, dimensions={0} | all-to-all | bytes 1835008 | tf_op jit(solution)/shard_map/all_to_all | solution.py:382
  133.4 0.2 reshape.69.g_ref
  133.6 0.0 copy-done.1
  133.6 21.5 %space_backward.1 = bf16[896,512]{1,0:T(8,128)(2,1)S(1)} custom-call(bf16[896,512]{1,0:T(8,128)(2,1)S(1)} %bitcast.20, f32[1,512]{1,0:T(1,128)S(1)} %bitcast.24, bf16[896,512]{1,0:T(8,128)(2,1)S(1)} %reshape.69.g_ref, bf16[896,512]{1,0:T(8,128)(2,1)} %copy-done.3, bf16[896,512]{1,0:T(8,128)(2,1)} %copy-done.4, bf16[896,512]{1,0:T(8,128)(2,1)} %get-tuple-element.14.v_ref, ...), custom_call_target="tpu_custom_call" | custom-call | tf_op jit(solution)/shard_map/space_backward/pallas_call | solution.py:295
  155.1 17.4 %all_to_all.34 = bf16[8,112,512]{2,1,0:T(8,128)(2,1)S(1)} all-to-all(bf16[8,112,512]{2,1,0:T(8,128)(2,1)S(1)} %bitcast.21), channel_id=1, replica_groups=mesh['round'=4,'stab'=8] {'stab'}, dimensions={0} | all-to-all | bytes 1835008 | tf_op jit(solution)/shard_map/all_to_all | solution.py:366
  172.6 1.5 convert_element_type.24
  (5 shorter events, 0.0 us)
Async XLA Ops:
  0.0 5.3 %copy-start.10 = (s32[8,112]{1,0:T(8,128)S(1)}, s32[8,112]{1,0:T(8,128)}, u32[]{:S(2)}) copy-start(s32[8,112]{1,0:T(8,128)} %param.11) | copy-start | bytes 10756
  0.0 23.4 %copy-start.9 = (s32[224,16]{0,1:T(8,128)S(1)}, s32[224,16]{0,1:T(8,128)}, u32[]{:S(2)}) copy-start(s32[224,16]{0,1:T(8,128)} %param.12) | copy-start | bytes 43012
  0.0 23.5 %copy-start.6 = (f32[512]{0:T(512)S(1)}, f32[512]{0:T(512)}, u32[]{:S(2)}) copy-start(f32[512]{0:T(512)} %param.15) | copy-start | bytes 6148
  0.0 23.5 %copy-start.2 = (bf16[512,512]{1,0:T(8,128)(2,1)S(1)}, bf16[512,512]{1,0:T(8,128)(2,1)}, u32[]{:S(2)}) copy-start(bf16[512,512]{1,0:T(8,128)(2,1)} %wo_ref.3) | copy-start | bytes 1572868
  0.0 19.3 %all-to-all-start = ((bf16[8,112,512]{2,1,0:T(8,128)(2,1)}), bf16[8,112,512]{2,1,0:T(8,128)(2,1)S(1)}, u32[]{:S(2)}, u32[]{:S(2)}) async-start(bf16[8,112,512]{2,1,0:T(8,128)(2,1)} %param.10), calls=%async_computation | async-start | bytes 1835008 | tf_op jit(solution)/shard_map/all_to_all | solution.py:362
  19.3 4.1 %copy-start = (bf16[8,112,512]{2,1,0:T(8,128)(2,1)}, bf16[8,112,512]{2,1,0:T(8,128)(2,1)S(1)}, u32[]{:S(2)}) copy-start(bf16[8,112,512]{2,1,0:T(8,128)(2,1)S(1)} %all-to-all-done) | copy-start | bytes 2752516
  19.3 33.9 %all-to-all-start.2 = ((s32[32,1,224]{2,1,0:T(1,128)}), s32[32,1,224]{2,1,0:T(1,128)S(1)}, u32[]{:S(2)}, u32[]{:S(2)}) async-start(s32[32,1,224]{2,1,0:T(1,128)} %all_to_all.24), calls=%async_computation.2 | async-start | bytes 65536 | tf_op jit(solution)/shard_map/all_to_all | solution.py:392
  50.2 1.0 copy-start.3
  51.2 0.9 copy-start.4
  53.2 32.1 %all-to-all-start.1 = ((bf16[32,28,512]{2,1,0:T(8,128)(2,1)}), bf16[32,28,512]{2,1,0:T(8,128)(2,1)S(1)}, u32[]{:S(2)}, u32[]{:S(2)}) async-start(bf16[32,28,512]{2,1,0:T(8,128)(2,1)} %reshape.61), calls=%async_computation.1 | async-start | bytes 2097152 | tf_op jit(solution)/shard_map/all_to_all | solution.py:374
  85.8 1.0 copy-start.5
  85.8 1.0 copy-start.7
  85.9 1.0 copy-start.8
  103.7 29.9 %copy-start.1 = (bf16[8,112,512]{2,1,0:T(8,128)(2,1)S(1)}, bf16[8,112,512]{2,1,0:T(8,128)(2,1)}, u32[]{:S(2)}) copy-start(bf16[8,112,512]{2,1,0:T(8,128)(2,1)} %copy-done) | copy-start | bytes 2752516

commit v3 on v2

--- a/solution.py
+++ b/solution.py
@@ -371,18 +371,32 @@
 
     def to_times(rows):
         if direct:
-            return lax.all_to_all(
-                rows.reshape(rounds, part, features), both, split_axis=0, concat_axis=0, tiled=True
-            )
+            split = rows.reshape(rounds, part, features)
+            return [
+                lax.all_to_all(split[:, piece], both, split_axis=0, concat_axis=0, tiled=True)
+                for piece in pieces
+            ]
         tokens = pad_stabs(to_tokens(rows))
-        return lax.all_to_all(tokens, "round", split_axis=1, concat_axis=0, tiled=True)
+        return [lax.all_to_all(tokens, "round", split_axis=1, concat_axis=0, tiled=True)]
 
     def from_times(times):
         if direct:
-            moved = lax.all_to_all(times, both, split_axis=0, concat_axis=0, tiled=True)
-            return moved.reshape(stabs, features)
-        tokens = lax.all_to_all(times, "round", split_axis=0, concat_axis=1, tiled=True)
+            moved = [
+                lax.all_to_all(piece, both, split_axis=0, concat_axis=0, tiled=True)
+                for piece in times
+            ]
+            return jnp.concatenate(moved, axis=1).reshape(stabs, features)
+        tokens = lax.all_to_all(times[0], "round", split_axis=0, concat_axis=1, tiled=True)
         return to_rounds(tokens[:, :stabs_here])
+
+    width = max(1, GROUP // rounds)
+    while part % width:
+        width -= 1
+    tokens = width * rounds
+    pieces = [slice(0, part)]
+    if direct and part > width:
+        middle = -(-part // (2 * width)) * width
+        pieces = [slice(0, middle), slice(middle, part)]
 
     here_round, here_stab = lax.axis_index("round"), lax.axis_index("stab")
     if direct:
@@ -407,30 +421,29 @@
         real = real & (slot < stabs_here)
     side = jnp.stack([targets, jnp.broadcast_to(real.astype(jnp.float32), targets.shape)], axis=-1)
 
-    width = max(1, GROUP // rounds)
-    while part % width:
-        width -= 1
-    groups = part // width
-    tokens = width * rounds
-
     def to_groups(times):
         depth = times.shape[-1]
-        split = times.reshape(rounds, groups, width, depth)
-        return jnp.transpose(split, (1, 0, 2, 3)).reshape(groups * tokens, depth)
+        split = times.reshape(rounds, -1, width, depth)
+        return jnp.transpose(split, (1, 0, 2, 3)).reshape(-1, depth)
 
     def from_groups(rows):
-        split = rows.reshape(groups, rounds, width, features)
-        return jnp.transpose(split, (1, 0, 2, 3)).reshape(rounds, part, features)
+        split = rows.reshape(-1, rounds, width, features)
+        return jnp.transpose(split, (1, 0, 2, 3)).reshape(rounds, -1, features)
 
     x = to_rounds(inputs)
     after_space, *saved = space_forward(
         x, neighbours, space_gain, space_in_weights, space_out_weights
     )
-    times = to_groups(to_times(after_space))
-    grad_times = time_both(
-        times, to_groups(side), time_gain, readout, time_in_weights, time_out_weights, width, tokens
-    )
-    grad_space = from_times(from_groups(grad_times))
+    grad_times = [
+        from_groups(
+            time_both(
+                to_groups(times), to_groups(side[:, piece]), time_gain, readout,
+                time_in_weights, time_out_weights, width, tokens,
+            )
+        )
+        for times, piece in zip(to_times(after_space), pieces)
+    ]
+    grad_space = from_times(grad_times)
     grad = space_backward(x, space_gain, grad_space, saved, space_in_weights, space_out_weights)
     return to_tokens(grad).astype(jnp.float32)
 

time: 174 us -> 175 us (level)
  blocking collectives: 47.1 us -> 35.2 us
  local copies, waits for them, and re-layouts: 7.24 us -> 14.8 us
  starting transfers between devices: 15.3 us -> 22 us
  waiting for transfers between devices: 38.4 us -> 35.1 us
  other arithmetic: 1.59 us -> 3.88 us
    all_to_all x1, blocking collectives: 29.7 us -> 18.3 us  [from_times(): lax.all_to_all(piece, both, split_axis=0, concat_axis=0, tiled=True)]
    all_to_all x1 -> x3, starting transfers between devices: 6.01 us -> 12.7 us  [the longest x2 9.36 us: to_times(): lax.all_to_all(split[:, piece], both, split_axis=0, concat_axis=0, tiled=...]
    all_to_all x1 -> x3, waiting for transfers between devices: 25.2 us -> 22.6 us  [the longest x2 19.4 us: to_times(): lax.all_to_all(split[:, piece], both, split_axis=0, concat_axis=0, tiled=...]
    unnamed x23 -> x25, local copies, waits for them, and re-layouts: 2.11 us -> 4.67 us
    concatenate x0 -> x1, other arithmetic: none -> 2.22 us  [from_times(): return jnp.concatenate(moved, axis=1).reshape(stabs, features)]
    slice x0 -> x4, local copies, waits for them, and re-layouts: none -> 1.84 us  [the longest x2 1.69 us: to_times(): split[:, piece]]
    pallas_call x1 -> x2, Pallas kernels: 15.9 us -> 15.1 us  [time_both(): pl.pallas_call(functools.partial(time_kernel, width), out_shape=jax.Shape...]
  transfers between devices with their start and end apart: 3 -> 5, of which waited for: 2 -> 4; matrix products, arithmetic and copies ran while one was open for 1% -> 5% of each run, Pallas kernels for 15% -> 24%
where the time goes in v3:
time: 175 us
  Pallas kernels  63.4 us (36%)
  blocking collectives  35.2 us (20%)
  waiting for transfers between devices  35.1 us (20%)
  starting transfers between devices  22 us (13%)
  local copies, waits for them, and re-layouts  14.8 us (8%)
  other arithmetic  3.88 us (2%)
    pallas_call x1, Pallas kernels, space_forward(): pl.pallas_call(space_forward_kernel, grid=(pairs,), in_specs=[whole(stabs...  26.7 us
    pallas_call x1, Pallas kernels, space_backward(): pl.pallas_call(space_backward_kernel, grid=(pairs,), in_specs=[whole(stab...  21.5 us
    all_to_all x2, waiting for transfers between devices, to_times(): lax.all_to_all(split[:, piece], both, split_axis=0, concat_axis=0, tiled=...  19.4 us
    all_to_all x1, blocking collectives, from_times(): lax.all_to_all(piece, both, split_axis=0, concat_axis=0, tiled=True)  18.3 us
    all_to_all x1, blocking collectives, to_tokens(): lax.all_to_all(split, 'stab', split_axis=0, concat_axis=0, tiled=True)  16.9 us
    pallas_call x2, Pallas kernels, time_both(): pl.pallas_call(functools.partial(time_kernel, width), out_shape=jax.Shape...  15.1 us
    all_to_all x1, waiting for transfers between devices, to_rounds(): lax.all_to_all(tokens, 'stab', split_axis=0, concat_axis=1, tiled=True)[0]  12.5 us
    all_to_all x2, starting transfers between devices, to_times(): lax.all_to_all(split[:, piece], both, split_axis=0, concat_axis=0, tiled=...  9.36 us
  transfers between devices with their start and end apart: 5, of which 4 were waited for; matrix products, arithmetic and copies ran while one was open for 5% of the time, Pallas kernels for 24%

profile of v3, /device:TPU:0, one launch (start us, length us, event | category | flops | bytes accessed | tf_op | source)
XLA Modules:
  0.0 174.6 jit_solution(3282451865474051151)
XLA Ops:
  0.0 0.0 copy-start.9
  0.0 0.0 copy-start.3
  0.0 5.3 %all-to-all-start = ((bf16[8,112,512]{2,1,0:T(8,128)(2,1)}), bf16[8,112,512]{2,1,0:T(8,128)(2,1)S(1)}, u32[]{:S(2)}, u32[]{:S(2)}) async-start(bf16[8,112,512]{2,1,0:T(8,128)(2,1)} %param.10), calls=%async_computation | async-start | bytes 1835008 | tf_op jit(solution)/shard_map/all_to_all | solution.py:362
  5.3 0.8 reshape.79
  6.1 0.1 tile.8
  6.2 0.7 all_to_all.30
  6.8 12.5 %all-to-all-done = bf16[8,112,512]{2,1,0:T(8,128)(2,1)S(1)} async-done(((bf16[8,112,512]{2,1,0:T(8,128)(2,1)}), bf16[8,112,512]{2,1,0:T(8,128)(2,1)S(1)}, u32[]{:S(2)}, u32[]{:S(2)}) %all-to-all-start) | async-done | bytes 917536 | tf_op jit(solution)/shard_map/all_to_all | solution.py:362
  19.3 0.0 copy-start
  19.3 4.0 %all-to-all-start.2 = ((s32[32,1,224]{2,1,0:T(1,128)}), s32[32,1,224]{2,1,0:T(1,128)S(1)}, u32[]{:S(2)}, u32[]{:S(2)}) async-start(s32[32,1,224]{2,1,0:T(1,128)} %all_to_all.30), calls=%async_computation.2 | async-start | bytes 65536 | tf_op jit(solution)/shard_map/all_to_all | solution.py:406
  23.3 0.8 copy.39.near_ref
  24.1 0.0 copy-done
  24.2 0.0 copy-done.9
  24.2 0.0 copy-done.3
  24.2 26.7 %space_forward.1 = (bf16[896,512]{1,0:T(8,128)(2,1)S(1)}, bf16[896,512]{1,0:T(8,128)(2,1)S(1)}, bf16[896,512]{1,0:T(8,128)(2,1)S(1)}, bf16[896,512]{1,0:T(8,128)...) custom-call(bf16[896,512]{1,0:T(8,128)(2,1)} %bitcast.28, s32[224,16]{1,0:T(8,128)S(1)} %copy.39.near_ref, ...), custom_call_target="tpu_custom_call" | custom-call | tf_op jit(solution)/shard_map/space_forward/pallas_call | solution.py:270
  50.9 0.0 copy-start.6
  50.9 0.9 copy-done.6
  51.8 0.0 copy-start.7
  51.8 0.9 copy-done.7
  52.8 0.2 reshape.76
  52.9 0.8 slice.19
  53.8 0.0 all-to-all-done.2
  53.8 5.8 %all-to-all-start.4 = ((bf16[32,12,512]{2,1,0:T(8,128)(2,1)}), bf16[32,12,512]{2,1,0:T(8,128)(2,1)S(1)}, u32[]{:S(2)}, u32[]{:S(2)}) async-start(bf16[32,12,512]{2,1,0:T(8,128)(2,1)} %slice.19), calls=%async_computation.4 | async-start | bytes 1048576 | tf_op jit(solution)/shard_map/all_to_all | solution.py:376
  59.6 0.8 slice.16
  60.5 14.7 %all-to-all-done.4 = bf16[32,12,512]{2,1,0:T(8,128)(2,1)S(1)} async-done(((bf16[32,12,512]{2,1,0:T(8,128)(2,1)}), bf16[32,12,512]{2,1,0:T(8,128)(2,1)S(1)}, u32[]{:S(2)}, u32[]{:S(2)}) %all-to-all-start.4) | async-done | bytes 393248 | tf_op jit(solution)/shard_map/all_to_all | solution.py:376
  75.2 3.5 %all-to-all-start.1 = ((bf16[32,16,512]{2,1,0:T(8,128)(2,1)}), bf16[32,16,512]{2,1,0:T(8,128)(2,1)}, u32[]{:S(2)}, u32[]{:S(2)}) async-start(bf16[32,16,512]{2,1,0:T(8,128)(2,1)} %slice.16), calls=%async_computation.1 | async-start | bytes 1048576 | tf_op jit(solution)/shard_map/all_to_all | solution.py:376
  78.7 0.1 reduce
  78.8 0.1 reshape.80
  78.9 0.1 pad_maximum_fusion.1
  79.0 0.1 copy.48
  79.1 0.8 copy.49
  79.9 0.2 copy.46
  80.2 0.3 copy.47
  80.5 0.1 reshape.86.h_ref
  80.6 0.0 copy-done.2
  80.6 0.0 copy-done.4
  80.6 0.0 copy-done.10
  80.6 0.0 copy-done.11
  80.6 0.0 copy-start.8
  80.6 0.9 copy-done.8
  81.6 6.6 %time_both.3 = bf16[384,512]{1,0:T(8,128)(2,1)S(1)} custom-call(bf16[384,512]{1,0:T(8,128)(2,1)S(1)} %reshape.86.h_ref, f32[384,2]{1,0:T(8,128)S(1)} %bitcast.32, f32[1,512]{1,0:T(1,128)S(1)} %bitcast.35, f32[1,512]{1,0:T(1,128)S(1)} %bitcast.37, bf16[512,1536]{1,0:T(8,128)(2,1)S(1)} %copy-done.2, bf16[512,512]{1,0:T(8,128)(2,1)S(1)} %copy-done.4), custom_call_target="tpu_custom_call" | custom-call | tf_op jit(solution)/shard_map/time_both/pallas_call | solution.py:319
  88.2 0.1 reshape.89
  88.3 0.1 copy.50
  88.3 1.0 copy.51
  89.4 4.7 %all-to-all-done.1 = bf16[32,16,512]{2,1,0:T(8,128)(2,1)} async-done(((bf16[32,16,512]{2,1,0:T(8,128)(2,1)}), bf16[32,16,512]{2,1,0:T(8,128)(2,1)}, u32[]{:S(2)}, u32[]{:S(2)}) %all-to-all-start.1) | async-done | bytes 524320 | tf_op jit(solution)/shard_map/all_to_all | solution.py:376
  94.0 3.3 %all-to-all-start.5 = ((bf16[32,12,512]{2,1,0:T(8,128)(2,1)}), bf16[32,12,512]{2,1,0:T(8,128)(2,1)}, u32[]{:S(2)}, u32[]{:S(2)}) async-start(bf16[32,12,512]{2,1,0:T(8,128)(2,1)} %copy.51), calls=%async_computation.5 | async-start | bytes 1048576 | tf_op jit(solution)/shard_map/all_to_all | solution.py:385
  97.4 0.1 copy.43
  97.5 0.2 copy.44
  97.7 1.3 copy.40
  99.0 0.4 copy.41
  99.4 0.1 reshape.78.h_ref
  99.5 0.0 copy-start.5
  99.6 1.0 copy-done.5
  100.6 8.5 %time_both.2 = bf16[512,512]{1,0:T(8,128)(2,1)S(1)} custom-call(bf16[512,512]{1,0:T(8,128)(2,1)S(1)} %reshape.78.h_ref, f32[512,2]{1,0:T(8,128)S(1)} %bitcast.31, f32[1,512]{1,0:T(1,128)S(1)} %bitcast.36, f32[1,512]{1,0:T(1,128)S(1)} %bitcast.38, bf16[512,1536]{1,0:T(8,128)(2,1)S(1)} %copy-done.2, bf16[512,512]{1,0:T(8,128)(2,1)S(1)} %copy-done.5), custom_call_target="tpu_custom_call" | custom-call | tf_op jit(solution)/shard_map/time_both/pallas_call | solution.py:319
  109.1 0.1 reshape.83
  109.3 0.3 copy.45
  109.5 0.1 reshape.84
  109.7 3.2 %all-to-all-done.5 = bf16[32,12,512]{2,1,0:T(8,128)(2,1)} async-done(((bf16[32,12,512]{2,1,0:T(8,128)(2,1)}), bf16[32,12,512]{2,1,0:T(8,128)(2,1)}, u32[]{:S(2)}, u32[]{:S(2)}) %all-to-all-start.5) | async-done | bytes 393248 | tf_op jit(solution)/shard_map/all_to_all | solution.py:385
  112.9 18.3 %all_to_all.43 = bf16[32,16,512]{2,1,0:T(8,128)(2,1)S(1)} all-to-all(bf16[32,16,512]{2,1,0:T(8,128)(2,1)S(1)} %reshape.84), channel_id=1, replica_groups=mesh['round'=4,'stab'=8] {'round','stab'}, dimensions={0} | all-to-all | bytes 1048576 | tf_op jit(solution)/shard_map/all_to_all | solution.py:385
  131.2 2.2 %pad_maximum_fusion = bf16[32,28,512]{2,1,0:T(8,128)(2,1)} fusion(bf16[32,12,512]{2,1,0:T(8,128)(2,1)} %all-to-all-done.5, bf16[32,16,512]{2,1,0:T(8,128)(2,1)S(1)} %all_to_all.43), kind=kLoop, calls=%fused_computation | loop fusion | flops 1835008 | bytes 1835008 | tf_op jit(solution)/shard_map/concatenate | solution.py:388
  133.4 1.3 reshape.91.g_ref
  134.7 0.0 copy-done.1
  134.8 21.5 %space_backward.1 = bf16[896,512]{1,0:T(8,128)(2,1)S(1)} custom-call(bf16[896,512]{1,0:T(8,128)(2,1)S(1)} %bitcast.29, f32[1,512]{1,0:T(1,128)S(1)} %bitcast.34, bf16[896,512]{1,0:T(8,128)(2,1)S(1)} %reshape.91.g_ref, bf16[896,512]{1,0:T(8,128)(2,1)} %copy-done.6, bf16[896,512]{1,0:T(8,128)(2,1)} %copy-done.7, bf16[896,512]{1,0:T(8,128)(2,1)} %get-tuple-element.14.v_ref, ...), custom_call_target="tpu_custom_call" | custom-call | tf_op jit(solution)/shard_map/space_backward/pallas_call | solution.py:295
  156.3 16.9 %all_to_all.44 = bf16[8,112,512]{2,1,0:T(8,128)(2,1)S(1)} all-to-all(bf16[8,112,512]{2,1,0:T(8,128)(2,1)S(1)} %bitcast.30), channel_id=1, replica_groups=mesh['round'=4,'stab'=8] {'stab'}, dimensions={0} | all-to-all | bytes 1835008 | tf_op jit(solution)/shard_map/all_to_all | solution.py:366
  173.2 1.5 convert_element_type.22
  (11 shorter events, 0.0 us)
Async XLA Ops:
  0.0 24.2 %copy-start.9 = (f32[512]{0:T(512)S(1)}, f32[512]{0:T(512)}, u32[]{:S(2)}) copy-start(f32[512]{0:T(512)} %param.15) | copy-start | bytes 6148
  0.0 24.2 %copy-start.3 = (bf16[512,512]{1,0:T(8,128)(2,1)S(1)}, bf16[512,512]{1,0:T(8,128)(2,1)}, u32[]{:S(2)}) copy-start(bf16[512,512]{1,0:T(8,128)(2,1)} %wo_ref.3) | copy-start | bytes 1572868
  0.0 19.3 %all-to-all-start = ((bf16[8,112,512]{2,1,0:T(8,128)(2,1)}), bf16[8,112,512]{2,1,0:T(8,128)(2,1)S(1)}, u32[]{:S(2)}, u32[]{:S(2)}) async-start(bf16[8,112,512]{2,1,0:T(8,128)(2,1)} %param.10), calls=%async_computation | async-start | bytes 1835008 | tf_op jit(solution)/shard_map/all_to_all | solution.py:362
  19.3 4.8 %copy-start = (bf16[8,112,512]{2,1,0:T(8,128)(2,1)}, bf16[8,112,512]{2,1,0:T(8,128)(2,1)S(1)}, u32[]{:S(2)}) copy-start(bf16[8,112,512]{2,1,0:T(8,128)(2,1)S(1)} %all-to-all-done) | copy-start | bytes 2752516
  19.3 34.5 %all-to-all-start.2 = ((s32[32,1,224]{2,1,0:T(1,128)}), s32[32,1,224]{2,1,0:T(1,128)S(1)}, u32[]{:S(2)}, u32[]{:S(2)}) async-start(s32[32,1,224]{2,1,0:T(1,128)} %all_to_all.30), calls=%async_computation.2 | async-start | bytes 65536 | tf_op jit(solution)/shard_map/all_to_all | solution.py:406
  50.9 0.9 copy-start.6
  51.8 0.9 copy-start.7
  53.8 21.4 %all-to-all-start.4 = ((bf16[32,12,512]{2,1,0:T(8,128)(2,1)}), bf16[32,12,512]{2,1,0:T(8,128)(2,1)S(1)}, u32[]{:S(2)}, u32[]{:S(2)}) async-start(bf16[32,12,512]{2,1,0:T(8,128)(2,1)} %slice.19), calls=%async_computation.4 | async-start | bytes 1048576 | tf_op jit(solution)/shard_map/all_to_all | solution.py:376
  60.5 20.1 %copy-start.2 = (bf16[512,1536]{1,0:T(8,128)(2,1)S(1)}, bf16[512,1536]{1,0:T(8,128)(2,1)}, u32[]{:S(2)}) copy-start(bf16[512,1536]{1,0:T(8,128)(2,1)} %win_ref.3) | copy-start | bytes 4718596
  60.5 20.1 %copy-start.4 = (bf16[512,512]{1,0:T(8,128)(2,1)S(1)}, bf16[512,512]{1,0:T(8,128)(2,1)}, u32[]{:S(2)}) copy-start(bf16[512,512]{1,0:T(8,128)(2,1)} %wout_ref.3) | copy-start | bytes 1572868
  60.5 20.1 %copy-start.10 = (f32[512]{0:T(512)S(1)}, f32[512]{0:T(512)}, u32[]{:S(2)}) copy-start(f32[512]{0:T(512)} %param.18) | copy-start | bytes 6148
  60.5 20.2 %copy-start.11 = (f32[512]{0:T(512)S(1)}, f32[512]{0:T(512)}, u32[]{:S(2)}) copy-start(f32[512]{0:T(512)} %param.19) | copy-start | bytes 6148
  75.2 18.9 %all-to-all-start.1 = ((bf16[32,16,512]{2,1,0:T(8,128)(2,1)}), bf16[32,16,512]{2,1,0:T(8,128)(2,1)}, u32[]{:S(2)}, u32[]{:S(2)}) async-start(bf16[32,16,512]{2,1,0:T(8,128)(2,1)} %slice.16), calls=%async_computation.1 | async-start | bytes 1048576 | tf_op jit(solution)/shard_map/all_to_all | solution.py:376
  80.6 0.9 copy-start.8
  94.0 18.9 %all-to-all-start.5 = ((bf16[32,12,512]{2,1,0:T(8,128)(2,1)}), bf16[32,12,512]{2,1,0:T(8,128)(2,1)}, u32[]{:S(2)}, u32[]{:S(2)}) async-start(bf16[32,12,512]{2,1,0:T(8,128)(2,1)} %copy.51), calls=%async_computation.5 | async-start | bytes 1048576 | tf_op jit(solution)/shard_map/all_to_all | solution.py:385
  99.5 1.0 copy-start.5
  131.2 3.5 %copy-start.1 = (bf16[8,112,512]{2,1,0:T(8,128)(2,1)S(1)}, bf16[8,112,512]{2,1,0:T(8,128)(2,1)}, u32[]{:S(2)}) copy-start(bf16[8,112,512]{2,1,0:T(8,128)(2,1)} %copy-done) | copy-start | bytes 2752516

commit v4 on v2

--- a/solution.py
+++ b/solution.py
@@ -12,8 +12,8 @@
 STABS_REAL = 840
 BLOCK = 4
 PAIR = 2 * HEAD_DIM
-CHUNK = 448
-BACK_CHUNK = 448
+CHUNK = 896
+BACK_CHUNK = 896
 GROUP = 128
 
 EPSILON = 1e-06
@@ -110,7 +110,7 @@
     step = pl.program_id(0)
     stabs = x_ref.shape[0]
     go = dot_nt(g_ref[...], wo_ref[...]).astype(jnp.bfloat16)
-    go_scr[...] = go
+    go_scr[...] = go * FACTOR
     product = go.astype(jnp.float32) * o_ref[...].astype(jnp.float32)
     q_turned = q_ref[...].T
     go_turned = go.T
@@ -118,13 +118,13 @@
         cols = slice(head * HEAD_DIM, (head + 1) * HEAD_DIM)
         keys = k_ref[:, cols]
         values = v_ref[:, cols]
-        delta = jnp.sum(product[:, cols], axis=-1, keepdims=True)
+        delta = jnp.sum(product[:, cols], axis=-1, keepdims=True) * FACTOR
         for start in range(0, stabs, BACK_CHUNK):
             rows = slice(start, start + BACK_CHUNK)
             grad_weights = dot_nt(go_scr[rows, cols], values)
             weights = p_ref[head, rows, :].astype(jnp.float32)
             grad_scores = (
-                weights * ((grad_weights - delta[start : start + BACK_CHUNK]) * FACTOR)
+                weights * (grad_weights - delta[start : start + BACK_CHUNK])
             ).astype(jnp.bfloat16)
             gs_scr[rows, :] = grad_scores
             dq_scr[rows, cols] = dot(grad_scores, keys).astype(jnp.bfloat16)

time: 174 us -> 175 us (level)
    pallas_call x1, Pallas kernels: 21.5 us -> 23.9 us  [space_backward(): pl.pallas_call(space_backward_kernel, grid=(pairs,), in_specs=[whole(stab...]
  transfers between devices with their start and end apart: 3 -> 3, of which waited for: 2 -> 2; matrix products, arithmetic and copies ran while one was open for 1% -> 1% of each run, Pallas kernels for 15% -> 14%
where the time goes in v4:
time: 175 us
  Pallas kernels  65.1 us (37%)
  blocking collectives  47.1 us (27%)
  waiting for transfers between devices  38.4 us (22%)
  starting transfers between devices  15.3 us (9%)
  local copies, waits for them, and re-layouts  7.24 us (4%)
    all_to_all x1, blocking collectives, from_times(): moved = lax.all_to_all(times, both, split_axis=0, concat_axis=0, tiled=True)  29.7 us
    pallas_call x1, Pallas kernels, space_forward(): pl.pallas_call(space_forward_kernel, grid=(pairs,), in_specs=[whole(stabs...  25.3 us
    all_to_all x1, waiting for transfers between devices, to_times(): lax.all_to_all(rows.reshape(rounds, part, features), both, split_axis=0,...  25.2 us
    pallas_call x1, Pallas kernels, space_backward(): pl.pallas_call(space_backward_kernel, grid=(pairs,), in_specs=[whole(stab...  23.9 us
    all_to_all x1, blocking collectives, to_tokens(): lax.all_to_all(split, 'stab', split_axis=0, concat_axis=0, tiled=True)  17.4 us
    pallas_call x1, Pallas kernels, time_both(): pl.pallas_call(functools.partial(time_kernel, width), out_shape=jax.Shape...  15.9 us
    all_to_all x1, waiting for transfers between devices, to_rounds(): lax.all_to_all(tokens, 'stab', split_axis=0, concat_axis=1, tiled=True)[0]  13.2 us
    all_to_all x1, starting transfers between devices, to_times(): lax.all_to_all(rows.reshape(rounds, part, features), both, split_axis=0,...  6.01 us
  transfers between devices with their start and end apart: 3, of which 2 were waited for; matrix products, arithmetic and copies ran while one was open for 1% of the time, Pallas kernels for 14%

profile of v4, /device:TPU:0, one launch (start us, length us, event | category | flops | bytes accessed | tf_op | source)
XLA Modules:
  0.0 175.0 jit_solution(16493003988992258786)
XLA Ops:
  0.0 0.0 copy-start.10
  0.0 0.0 copy-start.9
  0.0 0.0 copy-start.6
  0.0 0.0 copy-start.2
  0.0 5.3 %all-to-all-start = ((bf16[8,112,512]{2,1,0:T(8,128)(2,1)}), bf16[8,112,512]{2,1,0:T(8,128)(2,1)S(1)}, u32[]{:S(2)}, u32[]{:S(2)}) async-start(bf16[8,112,512]{2,1,0:T(8,128)(2,1)} %param.10), calls=%async_computation | async-start | bytes 1835008 | tf_op jit(solution)/shard_map/all_to_all | solution.py:362
  5.3 0.0 copy-done.10
  5.3 0.1 reshape.64
  5.4 0.1 tile.8
  5.5 0.6 all_to_all.24
  6.2 13.2 %all-to-all-done = bf16[8,112,512]{2,1,0:T(8,128)(2,1)S(1)} async-done(((bf16[8,112,512]{2,1,0:T(8,128)(2,1)}), bf16[8,112,512]{2,1,0:T(8,128)(2,1)S(1)}, u32[]{:S(2)}, u32[]{:S(2)}) %all-to-all-start) | async-done | bytes 917536 | tf_op jit(solution)/shard_map/all_to_all | solution.py:362
  19.3 0.0 copy-start
  19.3 4.0 %all-to-all-start.2 = ((s32[32,1,224]{2,1,0:T(1,128)}), s32[32,1,224]{2,1,0:T(1,128)S(1)}, u32[]{:S(2)}, u32[]{:S(2)}) async-start(s32[32,1,224]{2,1,0:T(1,128)} %all_to_all.24), calls=%async_computation.2 | async-start | bytes 65536 | tf_op jit(solution)/shard_map/all_to_all | solution.py:392
  23.4 0.0 copy-done.9
  23.4 0.1 copy.28.near_ref
  23.5 0.0 copy-done
  23.5 0.0 copy-done.6
  23.5 0.0 copy-done.2
  23.5 25.3 %space_forward.1 = (bf16[896,512]{1,0:T(8,128)(2,1)S(1)}, bf16[896,512]{1,0:T(8,128)(2,1)S(1)}, bf16[896,512]{1,0:T(8,128)(2,1)S(1)}, bf16[896,512]{1,0:T(8,128)...) custom-call(bf16[896,512]{1,0:T(8,128)(2,1)} %bitcast.19, s32[224,16]{1,0:T(8,128)S(1)} %copy.28.near_ref, ...), custom_call_target="tpu_custom_call" | custom-call | tf_op jit(solution)/shard_map/space_forward/pallas_call | solution.py:270
  48.7 0.0 copy-start.3
  48.7 1.0 copy-done.3
  49.7 0.0 copy-start.4
  49.7 0.9 copy-done.4
  50.6 1.1 reshape.61
  51.8 0.0 all-to-all-done.2
  51.8 6.0 %all-to-all-start.1 = ((bf16[32,28,512]{2,1,0:T(8,128)(2,1)}), bf16[32,28,512]{2,1,0:T(8,128)(2,1)S(1)}, u32[]{:S(2)}, u32[]{:S(2)}) async-start(bf16[32,28,512]{2,1,0:T(8,128)(2,1)} %reshape.61), calls=%async_computation.1 | async-start | bytes 2097152 | tf_op jit(solution)/shard_map/all_to_all | solution.py:374
  57.8 0.1 reduce
  57.9 0.1 reshape.65
  58.0 0.1 copy.32
  58.2 0.1 convert_element_type.22
  58.3 0.1 stack_broadcast_in_dim.3
  58.4 0.3 copy.33
  58.6 25.2 %all-to-all-done.1 = bf16[32,28,512]{2,1,0:T(8,128)(2,1)S(1)} async-done(((bf16[32,28,512]{2,1,0:T(8,128)(2,1)}), bf16[32,28,512]{2,1,0:T(8,128)(2,1)S(1)}, u32[]{:S(2)}, u32[]{:S(2)}) %all-to-all-start.1) | async-done | bytes 917536 | tf_op jit(solution)/shard_map/all_to_all | solution.py:374
  83.9 0.5 copy.29
  84.4 0.0 copy-start.5
  84.4 0.0 copy-start.7
  84.4 0.0 copy-start.8
  84.4 0.7 copy.30
  85.1 0.2 reshape.63.h_ref
  85.3 0.1 copy-done.5
  85.4 0.0 copy-done.7
  85.4 0.0 copy-done.8
  85.4 15.9 %time_both.1 = bf16[896,512]{1,0:T(8,128)(2,1)S(1)} custom-call(bf16[896,512]{1,0:T(8,128)(2,1)S(1)} %reshape.63.h_ref, f32[896,2]{1,0:T(8,128)S(1)} %bitcast.22, f32[1,512]{1,0:T(1,128)S(1)} %bitcast.25, f32[1,512]{1,0:T(1,128)S(1)} %bitcast.26, bf16[512,1536]{1,0:T(8,128)(2,1)} %win_ref.1, bf16[512,512]{1,0:T(8,128)(2,1)S(1)} %copy-done.5), custom_call_target="tpu_custom_call" | custom-call | tf_op jit(solution)/shard_map/time_both/pallas_call | solution.py:319
  101.3 0.2 reshape.67
  101.6 0.2 copy.34
  101.8 0.5 copy.35
  102.3 0.0 copy-start.1
  102.3 29.7 %all_to_all.33 = bf16[32,28,512]{2,1,0:T(8,128)(2,1)S(1)} all-to-all(bf16[32,28,512]{2,1,0:T(8,128)(2,1)S(1)} %copy.35), channel_id=1, replica_groups=mesh['round'=4,'stab'=8] {'round','stab'}, dimensions={0} | all-to-all | bytes 1835008 | tf_op jit(solution)/shard_map/all_to_all | solution.py:382
  131.9 0.2 reshape.69.g_ref
  132.1 0.0 copy-done.1
  132.1 23.9 %space_backward.1 = bf16[896,512]{1,0:T(8,128)(2,1)S(1)} custom-call(bf16[896,512]{1,0:T(8,128)(2,1)S(1)} %bitcast.20, f32[1,512]{1,0:T(1,128)S(1)} %bitcast.24, bf16[896,512]{1,0:T(8,128)(2,1)S(1)} %reshape.69.g_ref, bf16[896,512]{1,0:T(8,128)(2,1)} %copy-done.3, bf16[896,512]{1,0:T(8,128)(2,1)} %copy-done.4, bf16[896,512]{1,0:T(8,128)(2,1)} %get-tuple-element.14.v_ref, ...), custom_call_target="tpu_custom_call" | custom-call | tf_op jit(solution)/shard_map/space_backward/pallas_call | solution.py:295
  156.1 17.4 %all_to_all.34 = bf16[8,112,512]{2,1,0:T(8,128)(2,1)S(1)} all-to-all(bf16[8,112,512]{2,1,0:T(8,128)(2,1)S(1)} %bitcast.21), channel_id=1, replica_groups=mesh['round'=4,'stab'=8] {'stab'}, dimensions={0} | all-to-all | bytes 1835008 | tf_op jit(solution)/shard_map/all_to_all | solution.py:366
  173.5 1.5 convert_element_type.24
  (5 shorter events, 0.0 us)
Async XLA Ops:
  0.0 5.3 %copy-start.10 = (s32[8,112]{1,0:T(8,128)S(1)}, s32[8,112]{1,0:T(8,128)}, u32[]{:S(2)}) copy-start(s32[8,112]{1,0:T(8,128)} %param.11) | copy-start | bytes 10756
  0.0 23.4 %copy-start.9 = (s32[224,16]{0,1:T(8,128)S(1)}, s32[224,16]{0,1:T(8,128)}, u32[]{:S(2)}) copy-start(s32[224,16]{0,1:T(8,128)} %param.12) | copy-start | bytes 43012
  0.0 23.5 %copy-start.6 = (f32[512]{0:T(512)S(1)}, f32[512]{0:T(512)}, u32[]{:S(2)}) copy-start(f32[512]{0:T(512)} %param.15) | copy-start | bytes 6148
  0.0 23.5 %copy-start.2 = (bf16[512,512]{1,0:T(8,128)(2,1)S(1)}, bf16[512,512]{1,0:T(8,128)(2,1)}, u32[]{:S(2)}) copy-start(bf16[512,512]{1,0:T(8,128)(2,1)} %wo_ref.3) | copy-start | bytes 1572868
  0.0 19.3 %all-to-all-start = ((bf16[8,112,512]{2,1,0:T(8,128)(2,1)}), bf16[8,112,512]{2,1,0:T(8,128)(2,1)S(1)}, u32[]{:S(2)}, u32[]{:S(2)}) async-start(bf16[8,112,512]{2,1,0:T(8,128)(2,1)} %param.10), calls=%async_computation | async-start | bytes 1835008 | tf_op jit(solution)/shard_map/all_to_all | solution.py:362
  19.3 4.1 %copy-start = (bf16[8,112,512]{2,1,0:T(8,128)(2,1)}, bf16[8,112,512]{2,1,0:T(8,128)(2,1)S(1)}, u32[]{:S(2)}) copy-start(bf16[8,112,512]{2,1,0:T(8,128)(2,1)S(1)} %all-to-all-done) | copy-start | bytes 2752516
  19.3 32.4 %all-to-all-start.2 = ((s32[32,1,224]{2,1,0:T(1,128)}), s32[32,1,224]{2,1,0:T(1,128)S(1)}, u32[]{:S(2)}, u32[]{:S(2)}) async-start(s32[32,1,224]{2,1,0:T(1,128)} %all_to_all.24), calls=%async_computation.2 | async-start | bytes 65536 | tf_op jit(solution)/shard_map/all_to_all | solution.py:392
  48.7 1.0 copy-start.3
  49.7 0.9 copy-start.4
  51.8 32.1 %all-to-all-start.1 = ((bf16[32,28,512]{2,1,0:T(8,128)(2,1)}), bf16[32,28,512]{2,1,0:T(8,128)(2,1)S(1)}, u32[]{:S(2)}, u32[]{:S(2)}) async-start(bf16[32,28,512]{2,1,0:T(8,128)(2,1)} %reshape.61), calls=%async_computation.1 | async-start | bytes 2097152 | tf_op jit(solution)/shard_map/all_to_all | solution.py:374
  84.4 1.0 copy-start.5
  84.4 1.0 copy-start.7
  84.4 1.0 copy-start.8
  102.3 29.9 %copy-start.1 = (bf16[8,112,512]{2,1,0:T(8,128)(2,1)S(1)}, bf16[8,112,512]{2,1,0:T(8,128)(2,1)}, u32[]{:S(2)}) copy-start(bf16[8,112,512]{2,1,0:T(8,128)(2,1)} %copy-done) | copy-start | bytes 2752516
